TPU v7x, 32 devices: a whole 2x2x4 slice. The times are simulated.
32 devices in a mesh: mx: 8 (over z, core), my: 4 (over y, x).
Axes of the slice: x: 2, y: 2, z: 4, core: 2. Of those that a mesh axis runs over, the one named last changes fastest.
Arguments:
- features: bfloat16 [1024, 32, 512], P(('mx', 'my')), may hold values from -6 to 6
- coords: int32 [3, 1024], P(None, ('mx', 'my')), may hold values from 0 to 31, as said below
- counts: int32 [32], P(('mx', 'my')), may hold values from 16 to 32, as said below
- neighbours: int32 [6, 1024], P(None, ('mx', 'my')), may hold values from -1 to 1023, as said below
- fine_weights: bfloat16 [3, 32, 224], replicated, may hold values from -0.375 to 0.375
- down_weight: bfloat16 [2048, 256], replicated, may hold values from -0.25 to 0.25
- up_weight: bfloat16 [256, 2048], replicated, may hold values from -0.375 to 0.375
- norm_gain: float32 [256], replicated, may hold values from 0.1 to 1.9
- norm_bias: float32 [256], replicated, may hold values from -3 to 3
- coarse_weight: bfloat16 [6912, 256], P(None, 'my'), may hold values from -0.078125 to 0.078125
Outputs:
- fine_out: bfloat16 [1024, 32, 512], P(('mx', 'my'))
- coarse_out: bfloat16 [16, 8, 2, 256], P('mx', 'my')
Inputs may be any that keep to these rules, and one draw needn't show every extreme that they name: The live slots of a device are its first counts entries; some device is full in every draw. `coords`: the live blocks of the device with mx index i and my index j lie at z in [i * 4, (i + 1) * 4), y in [j * 4, (j + 1) * 4), x in [0, 4), distinct, in Morton order of their coordinates inside that region; slots that are not live hold 0. `neighbours`: A live block's entry is the slot of the live block one step away in that direction, or -1 if there is none; the relation is symmetric; slots that are not live hold -1.
All inputs are finite; a program needn't handle non-finite values.
Results may differ from a plain program's by a relative error of at most 0.0095.
Values may be sent and summed in bfloat16 or wider, within the bound.
A program may use at most 128 MiB of HBM per device.

v0:
```python
import jax
import jax.numpy as jnp
import numpy as np
from jax import lax
from jax.sharding import PartitionSpec as P

GROUPS = 32
SIDE = 8
RZ = 4
RY = 4
RX = 4


norm_eps = 1e-05


def padded_2(block, sides, width):
    for axis, dim in sides:
        count = lax.axis_size(axis)
        forward = [(i, i + 1) for i in range(count - 1)]
        backward = [(target, source) for source, target in forward]
        low = lax.ppermute(
            lax.slice_in_dim(block, block.shape[dim] - width, None, axis=dim), axis, forward
        )
        high = lax.ppermute(lax.slice_in_dim(block, 0, width, axis=dim), axis, backward)
        block = jnp.concatenate([low, block, high], axis=dim)
    return block


def displaced_taps(signal, near_blocks, block_side):
    volume = block_side * block_side * block_side
    voxel_ids = jnp.arange(volume, dtype=jnp.int32)
    along_x = voxel_ids % block_side
    along_y = voxel_ids // block_side % block_side
    along_z = voxel_ids // (block_side * block_side)
    last_layer = block_side - 1
    square = block_side * block_side
    plans = (
        (along_x < last_layer, -1, last_layer),
        (along_x > 0, 1, -last_layer),
        (along_y < last_layer, -block_side, block_side * last_layer),
        (along_y > 0, block_side, -block_side * last_layer),
        (along_z < last_layer, -square, square * last_layer),
        (along_z > 0, square, -square * last_layer),
    )
    tap_list = [signal]
    for (inside, own_shift, near_shift), block in zip(plans, near_blocks):
        tap_list.append(
            jnp.where(
                inside, jnp.roll(signal, own_shift, axis=2), jnp.roll(block, near_shift, axis=2)
            )
        )
    tap_stack = jnp.stack(tap_list, axis=1)
    return tap_stack.reshape(signal.shape[0], 7 * signal.shape[1], volume)


def coarse_patches(padded, depth, height, breadth):
    channel_count = padded.shape[3]
    pieces = []
    for step_z in range(3):
        for step_y in range(3):
            for step_x in range(3):
                pieces.append(
                    padded[
                        step_z : step_z + depth, step_y : step_y + height, step_x : step_x + breadth
                    ]
                )
    return jnp.stack(pieces, axis=3).reshape(depth * height * breadth, 27 * channel_count)


def face_tables(block_side):
    square = block_side * block_side
    last_layer = block_side - 1
    y_lower = np.array(
        [z * square + x for z in range(block_side) for x in range(block_side)], dtype=np.int32
    )
    z_lower = np.array(
        [y * block_side + x for y in range(block_side) for x in range(block_side)], dtype=np.int32
    )
    voxels = np.arange(square * block_side)
    along_x = voxels % block_side
    along_y = voxels // block_side % block_side
    along_z = voxels // square
    y_spread = (along_z * block_side + along_x).astype(np.int32)
    z_spread = (along_y * block_side + along_x).astype(np.int32)
    return (
        y_lower,
        y_lower + block_side * last_layer,
        z_lower,
        z_lower + square * last_layer,
        y_spread,
        z_spread,
    )


def fine_conv(signal, kernel_weight, layout):
    (
        slot_local,
        inside_rows,
        remote_rows,
        y_send_low,
        y_send_high,
        z_send_low,
        z_send_high,
        y_spot,
        z_spot,
    ) = layout
    block_count, chans, volume = signal.shape
    block_side = SIDE
    square = block_side * block_side
    face_size = chans * square
    y_lower, y_upper, z_lower, z_upper, y_spread, z_spread = face_tables(block_side)
    y_plane = jnp.zeros((2, RZ * RX, face_size), signal.dtype)
    y_plane = y_plane.at[0, y_send_low].set(
        signal[:, :, y_lower].reshape(block_count, face_size), mode="drop"
    )
    y_plane = y_plane.at[1, y_send_high].set(
        signal[:, :, y_upper].reshape(block_count, face_size), mode="drop"
    )
    z_plane = jnp.zeros((2, RY * RX, face_size), signal.dtype)
    z_plane = z_plane.at[0, z_send_low].set(
        signal[:, :, z_lower].reshape(block_count, face_size), mode="drop"
    )
    z_plane = z_plane.at[1, z_send_high].set(
        signal[:, :, z_upper].reshape(block_count, face_size), mode="drop"
    )
    y_rims = padded_2(y_plane, (("my", 0),), 1)
    z_rims = padded_2(z_plane, (("mx", 0),), 1)
    face_shape = (block_count, chans, square)
    stand_ins = (
        None,
        None,
        y_rims[3][y_spot].reshape(face_shape)[:, :, y_spread],
        y_rims[0][y_spot].reshape(face_shape)[:, :, y_spread],
        z_rims[3][z_spot].reshape(face_shape)[:, :, z_spread],
        z_rims[0][z_spot].reshape(face_shape)[:, :, z_spread],
    )
    near_blocks = []
    for direction in range(6):
        picked = signal[slot_local[direction]]
        block = jnp.where(inside_rows[direction][:, None, None], picked, jnp.zeros_like(picked))
        if stand_ins[direction] is not None:
            block = jnp.where(remote_rows[direction][:, None, None], stand_ins[direction], block)
        near_blocks.append(block)
    tap_stack = displaced_taps(signal, near_blocks, block_side)
    return jnp.einsum("pn,enh->eph", kernel_weight, tap_stack, preferred_element_type=jnp.float32)


def residual_step(base, kernel_weight, layout):
    signal = jax.nn.silu(base.astype(jnp.float32)).astype(jnp.bfloat16)
    return (base.astype(jnp.float32) + fine_conv(signal, kernel_weight, layout)).astype(
        jnp.bfloat16
    )


def octant_table(block_side):
    half_side = block_side // 2
    voxels = jnp.arange(block_side * block_side * block_side, dtype=jnp.int32)
    along_x = voxels % block_side
    along_y = voxels // block_side % block_side
    along_z = voxels // (block_side * block_side)
    octant = along_z // half_side * 4 + along_y // half_side * 2 + along_x // half_side
    return octant[:, None] == jnp.arange(8, dtype=jnp.int32)[None, :]


def local(
    features,
    coords,
    counts,
    neighbours,
    fine_weights,
    down_weight,
    up_weight,
    norm_gain,
    norm_bias,
    coarse_weight,
):
    block_count, chans, volume = features.shape
    major = lax.axis_index("mx")
    minor = lax.axis_index("my")
    across = lax.axis_size("my")
    first_slot = (major * across + minor) * block_count
    is_live = jnp.arange(block_count, dtype=jnp.int32) < counts[0]
    local_z = coords[0] - major * RZ
    local_y = coords[1] - minor * RY
    column_x = coords[2]
    slot_local = []
    inside_rows = []
    remote_rows = []
    for direction in range(6):
        target_slot = neighbours[direction] - first_slot
        present = neighbours[direction] >= 0
        here = present & (target_slot >= 0) & (target_slot < block_count)
        slot_local.append(jnp.clip(target_slot, 0, block_count - 1))
        inside_rows.append(here)
        remote_rows.append(present & jnp.logical_not(here))
    y_index = local_z * RX + column_x
    z_index = local_y * RX + column_x
    y_send_low = jnp.where(is_live & (local_y == 0), y_index, RZ * RX)
    y_send_high = jnp.where(is_live & (local_y == RY - 1), y_index, RZ * RX)
    z_send_low = jnp.where(is_live & (local_z == 0), z_index, RY * RX)
    z_send_high = jnp.where(is_live & (local_z == RZ - 1), z_index, RY * RX)
    layout = (
        slot_local,
        inside_rows,
        remote_rows,
        y_send_low,
        y_send_high,
        z_send_low,
        z_send_high,
        jnp.clip(y_index, 0, RZ * RX - 1),
        jnp.clip(z_index, 0, RY * RX - 1),
    )
    first_level = residual_step(features, fine_weights[0], layout)
    octant_hits = octant_table(SIDE)
    pool_matrix = octant_hits.astype(jnp.bfloat16) * jnp.asarray(1.0 / 64.0, jnp.bfloat16)
    pooled = jnp.dot(
        first_level.reshape(block_count * chans, volume),
        pool_matrix,
        preferred_element_type=jnp.float32,
    )
    pooled = (
        pooled.reshape(block_count, chans, 8)
        .transpose(0, 2, 1)
        .reshape(block_count, 8 * chans)
        .astype(jnp.bfloat16)
    )
    depth = RZ // 2
    height = RY // 2
    breadth = RX // 2
    cell_count = depth * height * breadth
    cell_ids = (local_z // 2 * height + local_y // 2) * breadth + column_x // 2
    octant_pos = local_z % 2 * 4 + local_y % 2 * 2 + column_x % 2
    target = jnp.where(is_live, cell_ids * 8 + octant_pos, cell_count * 8)
    gathered = (
        jnp.zeros((cell_count * 8, 8 * chans), jnp.bfloat16).at[target].set(pooled, mode="drop")
    )
    coarse_in = jnp.dot(
        gathered.reshape(cell_count, 64 * chans), down_weight, preferred_element_type=jnp.float32
    )
    coarse_width = coarse_in.shape[1]
    group_size = coarse_width // GROUPS
    grouped = coarse_in.reshape(cell_count, GROUPS, group_size)
    entries = cell_count * group_size * lax.axis_size("mx") * across
    first_sum, second_sum = lax.psum(
        (jnp.sum(grouped, axis=(0, 2)), jnp.sum(grouped * grouped, axis=(0, 2))), ("mx", "my")
    )
    group_mean = first_sum / entries
    variance = second_sum / entries - group_mean * group_mean
    normed = (
        (grouped - group_mean[None, :, None]) / jnp.sqrt(variance + norm_eps)[None, :, None]
    ).reshape(cell_count, coarse_width)
    normed = normed * norm_gain + norm_bias
    activated = (
        jax.nn.silu(normed).astype(jnp.bfloat16).reshape(depth, height, breadth, coarse_width)
    )
    padded = padded_2(activated, (("mx", 0), ("my", 1)), 1)
    padded = jnp.pad(padded, ((0, 0), (0, 0), (1, 1), (0, 0)))
    columns = coarse_patches(padded, depth, height, breadth)
    convolution_result = jnp.dot(
        columns,
        lax.all_gather(coarse_weight, "my", axis=1, tiled=True),
        preferred_element_type=jnp.float32,
    )
    coarse_out = (convolution_result + coarse_in).astype(jnp.bfloat16)
    lifted = jnp.dot(coarse_out, up_weight, preferred_element_type=jnp.float32).reshape(
        cell_count * 8, 8 * chans
    )
    per_block = lifted[jnp.clip(target, 0, cell_count * 8 - 1)]
    per_block = jnp.where(is_live[:, None], per_block, jnp.zeros_like(per_block))
    octant_values = (
        per_block.reshape(block_count, 8, chans).transpose(0, 2, 1).reshape(block_count * chans, 8)
    )
    spread_matrix = octant_hits.astype(jnp.float32).T
    spread_up = jnp.dot(
        octant_values,
        spread_matrix,
        precision=lax.Precision.HIGHEST,
        preferred_element_type=jnp.float32,
    )
    merged_features = (
        first_level.astype(jnp.float32) + spread_up.reshape(block_count, chans, volume)
    ).astype(jnp.bfloat16)
    second_level = residual_step(merged_features, fine_weights[1], layout)
    final_level = residual_step(second_level, fine_weights[2], layout)
    fine_out = jnp.where(is_live[:, None, None], final_level, jnp.zeros_like(final_level))
    return (fine_out, coarse_out.reshape(depth, height, breadth, coarse_width))


def solution(mesh):
    in_specs = (
        P(("mx", "my"), None, None),
        P(None, ("mx", "my")),
        P(("mx", "my")),
        P(None, ("mx", "my")),
        P(),
        P(),
        P(),
        P(),
        P(),
        P(None, "my"),
    )
    out_specs = (P(("mx", "my"), None, None), P("mx", "my", None, None))
    return jax.shard_map(local, mesh=mesh, in_specs=in_specs, out_specs=out_specs, check_vma=False)
```

profile of v0, /device:TPU:3, one launch (start us, length us, event | category | flops | bytes accessed | tf_op | source)
XLA Modules:
  0.0 590.1 jit_solution(9406478948444150339)
XLA Ops:
  9.9 6.5 %copy.144 = bf16[32,32,512]{1,0,2:T(8,128)(2,1)} copy(bf16[32,32,512]{2,1,0:T(8,128)(2,1)S(1)} %fusion.3) | data formatting | bytes 2097152 | tf_op jit(solution)/shard_map/convert_element_type | solution.py:150
  35.1 4.3 collective-permute-start.1
  48.2 4.7 scatter_fusion.2
  52.9 4.7 scatter_fusion.3
  96.4 3.8 fusion.18
  104.4 3.8 gather_fusion.5
  108.2 5.3 copy.149
  122.5 5.3 copy.151
  137.2 5.3 copy.157
  151.8 4.6 copy.159
  167.4 4.5 copy.160
  177.7 38.2 %all-reduce.5 = (f32[32]{0:T(128)S(1)}, f32[32]{0:T(128)S(1)}) all-reduce(f32[32]{0:T(128)S(1)} %reduce_sum.37, f32[32]{0:T(128)S(1)} %reduce_sum.25), channel_id=1, replica_groups=mesh['mx'=8,'my'=4] {'mx','my'}, use_global_device_ids=true, to_apply=%region_10.11 | all-reduce | flops 64 | bytes 512 | tf_op jit(solution)/shard_map/psum | solution.py:245
  216.3 4.0 collective-permute-start.4
  227.3 4.3 collective-permute-start.6
  233.0 33.4 %all-gather.2.cloned.1.call-done = bf16[6912,256]{0,1:T(8,128)(2,1)} async-done(((bf16[6912,64]{0,1:T(8,128)(2,1)}), bf16[6912,256]{0,1:T(8,128)(2,1)}) %all-gather.2.cloned.1.call-update) | async-done | bytes 3538960 | tf_op jit(solution)/shard_map/all_gather | solution.py:262
  286.3 6.9 %copy.164 = bf16[32,32,512]{1,0,2:T(8,128)(2,1)} copy(bf16[32,32,512]{2,1,0:T(8,128)(2,1)S(1)} %fusion.8) | data formatting | bytes 2097152 | tf_op jit(solution)/shard_map/convert_element_type | solution.py:150
  303.5 3.8 gather_fusion.29
  353.2 4.0 collective-permute-start.9
  362.6 4.4 copy.169
  375.8 4.4 copy.171
  389.3 4.4 copy.177
  402.8 4.6 copy.179
  417.2 4.6 copy.180
  437.4 6.8 %copy.183 = bf16[32,32,512]{1,0,2:T(8,128)(2,1)} copy(bf16[32,32,512]{2,1,0:T(8,128)(2,1)S(1)} %fusion.13) | data formatting | bytes 2097152 | tf_op jit(solution)/shard_map/convert_element_type | solution.py:150
  475.1 4.7 scatter_fusion.9
  489.9 4.7 scatter_fusion.11
  509.8 4.4 collective-permute-start.13
  519.6 4.4 copy.188
  532.8 4.4 copy.190
  546.3 4.4 copy.196
  559.7 4.6 copy.198
  575.3 4.5 copy.199
  (615 shorter events, 360.2 us)
Async XLA Ops:
  7.2 262.3 %copy-start = (bf16[256,2048]{1,0:T(8,128)(2,1)S(1)}, bf16[256,2048]{1,0:T(8,128)(2,1)}, u32[]{:S(2)}) copy-start(bf16[256,2048]{1,0:T(8,128)(2,1)} %param.58) | copy-start | bytes 3145732
  7.2 259.3 %all-gather.2.cloned.1.call-start = ((), (), s32[]{:S(2)}) async-start(), calls=%async_computation | async-start | bytes 4423680 | tf_op jit(solution)/shard_map/all_gather | solution.py:262
  25.6 13.8 %copy-start.140 = (s32[64]{0:T(128)S(1)}, s32[64]{0:T(128)}, u32[]{:S(2)}) copy-start(s32[64]{0:T(128)} %constant.466) | copy-start | bytes 772
  33.2 69.4 %collective-permute-start = (bf16[1,16,2048]{2,1,0:T(8,128)(2,1)}, bf16[1,16,2048]{2,1,0:T(8,128)(2,1)S(1)}, u32[]{:S(2)}, u32[]{:S(2)}) collective-permute-start(bf16[1,16,2048]{2,1,0:T(8,128)(2,1)} %get-tuple-element.65), channel_id=1, source_target_pairs={{1,0},{2,1},{3,2},{5,4},{6,5},{7,6},{9,8},{10,9},{11,10},{13,12},{... | collective-permute-start | bytes 196616 | tf_op jit(solution)/shard_map/ppermute | solution.py:25
  35.1 82.0 %collective-permute-start.1 = (bf16[1,16,2048]{2,1,0:T(8,128)(2,1)}, bf16[1,16,2048]{2,1,0:T(8,128)(2,1)S(1)}, u32[]{:S(2)}, u32[]{:S(2)}) collective-permute-start(bf16[1,16,2048]{2,1,0:T(8,128)(2,1)} %get-tuple-element.64), channel_id=1, source_target_pairs={{0,1},{1,2},{2,3},{4,5},{5,6},{6,7},{8,9},{9,10},{10,11},{12,13},{... | collective-permute-start | bytes 196616 | tf_op jit(solution)/shard_map/ppermute | solution.py:22
  39.4 13.5 %copy-start.104 = (s32[1024]{0:T(1024)}, s32[1024]{0:T(1024)S(1)}, u32[]{:S(2)}) copy-start(s32[1024]{0:T(1024)S(1)} %get-tuple-element.106) | copy-start | bytes 12292
  39.4 13.5 %copy-start.105 = (s32[1024]{0:T(1024)}, s32[1024]{0:T(1024)S(1)}, u32[]{:S(2)}) copy-start(s32[1024]{0:T(1024)S(1)} %get-tuple-element.107) | copy-start | bytes 12292
  48.2 17.4 %copy-start.2 = (bf16[32,32,512]{2,1,0:T(8,128)(2,1)S(1)}, bf16[32,32,512]{2,1,0:T(8,128)(2,1)}, u32[]{:S(2)}) copy-start(bf16[32,32,512]{2,1,0:T(8,128)(2,1)} %param.52) | copy-start | bytes 3145732
  58.2 73.5 %collective-permute-start.2 = (bf16[1,16,2048]{2,1,0:T(8,128)(2,1)}, bf16[1,16,2048]{2,1,0:T(8,128)(2,1)S(1)}, u32[]{:S(2)}, u32[]{:S(2)}) collective-permute-start(bf16[1,16,2048]{2,1,0:T(8,128)(2,1)} %get-tuple-element.63), channel_id=1, source_target_pairs={{4,0},{8,4},{12,8},{16,12},{20,16},{24,20},{28,24},{5,1},{9,5},{13... | collective-permute-start | bytes 196616 | tf_op jit(solution)/shard_map/ppermute | solution.py:25
  61.4 85.1 %collective-permute-start.3 = (bf16[1,16,2048]{2,1,0:T(8,128)(2,1)}, bf16[1,16,2048]{2,1,0:T(8,128)(2,1)S(1)}, u32[]{:S(2)}, u32[]{:S(2)}) collective-permute-start(bf16[1,16,2048]{2,1,0:T(8,128)(2,1)} %get-tuple-element.62), channel_id=1, source_target_pairs={{0,4},{4,8},{8,12},{12,16},{16,20},{20,24},{24,28},{1,5},{5,9},{9,... | collective-permute-start | bytes 196616 | tf_op jit(solution)/shard_map/ppermute | solution.py:22
  75.0 21.4 %copy-start.124 = (pred[512]{0:T(512)(128)(4,1)}, pred[512]{0:T(512)(128)(4,1)S(1)}, u32[]{:S(2)}) copy-start(pred[512]{0:T(512)(128)(4,1)S(1)} %fusion.85) | copy-start | bytes 1540
  80.2 19.9 %copy-start.127 = (pred[512]{0:T(512)(128)(4,1)}, pred[512]{0:T(512)(128)(4,1)S(1)}, u32[]{:S(2)}) copy-start(pred[512]{0:T(512)(128)(4,1)S(1)} %fusion.84) | copy-start | bytes 1540
  174.0 42.2 %copy-start.136 = (f32[256]{0:T(256)S(1)}, f32[256]{0:T(256)}, u32[]{:S(2)}) copy-start(f32[256]{0:T(256)} %param.60) | copy-start | bytes 3076
  174.0 42.2 %copy-start.137 = (f32[256]{0:T(256)S(1)}, f32[256]{0:T(256)}, u32[]{:S(2)}) copy-start(f32[256]{0:T(256)} %param.59) | copy-start | bytes 3076
  216.3 6.0 %collective-permute-start.4 = (bf16[1,2,2,256]{3,2,1,0:T(2,128)(2,1)S(1)}, bf16[1,2,2,256]{3,2,1,0:T(2,128)(2,1)S(1)}, u32[]{:S(2)}, u32[]{:S(2)}) collective-permute-start(bf16[1,2,2,256]{3,2,1,0:T(2,128)(2,1)S(1)} %slice.474), channel_id=1, source_target_pairs={{0,4},{4,8},{8,12},{12,16},{16,20},{20,24},{24,28},{1,5},{5,9},{9,... | collective-permute-start | bytes 6152 | tf_op jit(solution)/shard_map/ppermute | solution.py:22
  220.5 4.9 collective-permute-start.5
  225.4 6.2 %collective-permute-start.7 = (bf16[4,1,2,256]{3,2,1,0:T(2,128)(2,1)S(1)}, bf16[4,1,2,256]{3,2,1,0:T(2,128)(2,1)S(1)}, u32[]{:S(2)}, u32[]{:S(2)}) collective-permute-start(bf16[4,1,2,256]{3,2,1,0:T(2,128)(2,1)S(1)} %get-tuple-element.67), channel_id=1, source_target_pairs={{1,0},{2,1},{3,2},{5,4},{6,5},{7,6},{9,8},{10,9},{11,10},{13,12},{... | collective-permute-start | bytes 12296 | tf_op jit(solution)/shard_map/ppermute | solution.py:25
  227.3 5.1 collective-permute-start.6
  231.6 39.0 %copy-start.138 = (pred[32]{0:T(512)(128)(4,1)}, pred[32]{0:T(512)(128)(4,1)S(1)}, u32[]{:S(2)}) copy-start(pred[32]{0:T(512)(128)(4,1)S(1)} %iota_compare_fusion.4) | copy-start | bytes 100
  325.3 31.9 %collective-permute-start.8 = (bf16[1,16,2048]{2,1,0:T(8,128)(2,1)S(1)}, bf16[1,16,2048]{2,1,0:T(8,128)(2,1)S(1)}, u32[]{:S(2)}, u32[]{:S(2)}) collective-permute-start(bf16[1,16,2048]{2,1,0:T(8,128)(2,1)S(1)} %get-tuple-element.61), channel_id=1, source_target_pairs={{1,0},{2,1},{3,2},{5,4},{6,5},{7,6},{9,8},{10,9},{11,10},{13,12},{... | collective-permute-start | bytes 196616 | tf_op jit(solution)/shard_map/ppermute | solution.py:25
  330.2 14.0 %copy-start.34 = (bf16[32,1,32,7]{3,2,0,1:T(8,128)(2,1)S(1)}, bf16[32,1,32,7]{3,2,0,1:T(8,128)(2,1)}, u32[]{:S(2)}) copy-start(bf16[32,1,32,7]{3,2,0,1:T(8,128)(2,1)} %slice_bitcast_fusion.58) | copy-start | bytes 43012
  330.2 14.0 %copy-start.60 = (bf16[32,1,32,1]{3,2,0,1:T(8,128)(2,1)S(1)}, bf16[32,1,32,1]{3,2,0,1:T(8,128)(2,1)}, u32[]{:S(2)}) copy-start(bf16[32,1,32,1]{3,2,0,1:T(8,128)(2,1)} %get-tuple-element.39) | copy-start | bytes 6148
  337.1 10.6 %copy-start.5 = (bf16[32,1,32,505]{3,2,0,1:T(8,128)(2,1)S(1)}, bf16[32,1,32,505]{3,2,0,1:T(8,128)(2,1)}, u32[]{:S(2)}) copy-start(bf16[32,1,32,505]{3,2,0,1:T(8,128)(2,1)} %slice_bitcast_fusion.20) | copy-start | bytes 3102724
  337.9 46.0 %collective-permute-start.10 = (bf16[1,16,2048]{2,1,0:T(8,128)(2,1)}, bf16[1,16,2048]{2,1,0:T(8,128)(2,1)S(1)}, u32[]{:S(2)}, u32[]{:S(2)}) collective-permute-start(bf16[1,16,2048]{2,1,0:T(8,128)(2,1)} %get-tuple-element.59), channel_id=1, source_target_pairs={{4,0},{8,4},{12,8},{16,12},{20,16},{24,20},{28,24},{5,1},{9,5},{13... | collective-permute-start | bytes 196616 | tf_op jit(solution)/shard_map/ppermute | solution.py:25
  341.0 56.3 %collective-permute-start.11 = (bf16[1,16,2048]{2,1,0:T(8,128)(2,1)}, bf16[1,16,2048]{2,1,0:T(8,128)(2,1)S(1)}, u32[]{:S(2)}, u32[]{:S(2)}) collective-permute-start(bf16[1,16,2048]{2,1,0:T(8,128)(2,1)} %get-tuple-element.58), channel_id=1, source_target_pairs={{0,4},{4,8},{8,12},{12,16},{16,20},{20,24},{24,28},{1,5},{5,9},{9,... | collective-permute-start | bytes 196616 | tf_op jit(solution)/shard_map/ppermute | solution.py:22
  353.2 17.2 %collective-permute-start.9 = (bf16[1,16,2048]{2,1,0:T(8,128)(2,1)}, bf16[1,16,2048]{2,1,0:T(8,128)(2,1)S(1)}, u32[]{:S(2)}, u32[]{:S(2)}) collective-permute-start(bf16[1,16,2048]{2,1,0:T(8,128)(2,1)} %get-tuple-element.60), channel_id=1, source_target_pairs={{0,1},{1,2},{2,3},{4,5},{5,6},{6,7},{8,9},{9,10},{10,11},{12,13},{... | collective-permute-start | bytes 196616 | tf_op jit(solution)/shard_map/ppermute | solution.py:22
  480.4 33.8 %collective-permute-start.12 = (bf16[1,16,2048]{2,1,0:T(8,128)(2,1)}, bf16[1,16,2048]{2,1,0:T(8,128)(2,1)S(1)}, u32[]{:S(2)}, u32[]{:S(2)}) collective-permute-start(bf16[1,16,2048]{2,1,0:T(8,128)(2,1)} %get-tuple-element.57), channel_id=1, source_target_pairs={{1,0},{2,1},{3,2},{5,4},{6,5},{7,6},{9,8},{10,9},{11,10},{13,12},{... | collective-permute-start | bytes 196616 | tf_op jit(solution)/shard_map/ppermute | solution.py:25
  486.4 14.6 %copy-start.3 = (bf16[32,1,32,505]{3,2,0,1:T(8,128)(2,1)S(1)}, bf16[32,1,32,505]{3,2,0,1:T(8,128)(2,1)}, u32[]{:S(2)}) copy-start(bf16[32,1,32,505]{3,2,0,1:T(8,128)(2,1)} %slice_bitcast_fusion.10) | copy-start | bytes 3102724
  486.4 14.6 %copy-start.126 = (pred[512]{0:T(512)(128)(4,1)S(1)}, pred[512]{0:T(512)(128)(4,1)}, u32[]{:S(2)}) copy-start(pred[512]{0:T(512)(128)(4,1)} %copy-done.124) | copy-start | bytes 1540
  495.3 45.6 %collective-permute-start.14 = (bf16[1,16,2048]{2,1,0:T(8,128)(2,1)}, bf16[1,16,2048]{2,1,0:T(8,128)(2,1)S(1)}, u32[]{:S(2)}, u32[]{:S(2)}) collective-permute-start(bf16[1,16,2048]{2,1,0:T(8,128)(2,1)} %get-tuple-element.55), channel_id=1, source_target_pairs={{4,0},{8,4},{12,8},{16,12},{20,16},{24,20},{28,24},{5,1},{9,5},{13... | collective-permute-start | bytes 196616 | tf_op jit(solution)/shard_map/ppermute | solution.py:25
  497.3 57.0 %collective-permute-start.15 = (bf16[1,16,2048]{2,1,0:T(8,128)(2,1)S(1)}, bf16[1,16,2048]{2,1,0:T(8,128)(2,1)S(1)}, u32[]{:S(2)}, u32[]{:S(2)}) collective-permute-start(bf16[1,16,2048]{2,1,0:T(8,128)(2,1)S(1)} %get-tuple-element.54), channel_id=1, source_target_pairs={{0,4},{4,8},{8,12},{12,16},{16,20},{20,24},{24,28},{1,5},{5,9},{9,... | collective-permute-start | bytes 196616 | tf_op jit(solution)/shard_map/ppermute | solution.py:22
  509.8 17.6 %collective-permute-start.13 = (bf16[1,16,2048]{2,1,0:T(8,128)(2,1)S(1)}, bf16[1,16,2048]{2,1,0:T(8,128)(2,1)S(1)}, u32[]{:S(2)}, u32[]{:S(2)}) collective-permute-start(bf16[1,16,2048]{2,1,0:T(8,128)(2,1)S(1)} %get-tuple-element.56), channel_id=1, source_target_pairs={{0,1},{1,2},{2,3},{4,5},{5,6},{6,7},{8,9},{9,10},{10,11},{12,13},{... | collective-permute-start | bytes 196616 | tf_op jit(solution)/shard_map/ppermute | solution.py:22
  (128 other events, 488.7 us)
Sparse Core Ops, SparseCore 0:
  220.5 45.8 all-gather.1
where the time goes:
time: 602 us; the launch traced here: 590 us
  local copies, waits for them, and re-layouts  359 us (60%)
  other arithmetic  71.5 us (12%)
  starting transfers between devices  49.6 us (8%)
  blocking collectives  38.2 us (6%)
  waiting for transfers between devices  37.2 us (6%)
  between operations  17.5 us (3%)
  matrix products  17.1 us (3%)
    psum x1, blocking collectives, local(): lax.psum((jnp.sum(grouped, axis=(0, 2)), jnp.sum(grouped * grouped, axis=...  38.2 us
    unnamed x24, other arithmetic  34.1 us
    all_gather x1, waiting for transfers between devices, local(): lax.all_gather(coarse_weight, 'my', axis=1, tiled=True)  33.4 us
    concatenate x36, local copies, waits for them, and re-layouts, displaced_taps(): jnp.roll(block, near_shift, axis=2)  31.5 us
    ppermute x8, starting transfers between devices, padded_2(): lax.ppermute(lax.slice_in_dim(block, block.shape[dim] - width, None, axis...  31.4 us
    gather x9, local copies, waits for them, and re-layouts, fine_conv(): y_rims[3][y_spot].reshape(face_shape)[:, :, y_spread]  27.4 us
    gather x9, local copies, waits for them, and re-layouts, fine_conv(): z_rims[3][z_spot].reshape(face_shape)[:, :, z_spread]  27.2 us
    gather x9, local copies, waits for them, and re-layouts, fine_conv(): y_rims[0][y_spot].reshape(face_shape)[:, :, y_spread]  27.2 us
  transfers between devices with their start and end apart: 17, of which 3 were waited for; matrix products, arithmetic and copies ran while one was open for 37% of the time, Pallas kernels for 0%

commit v1 on v0

v1 whole, which is shorter than its diff:
```python
import functools

import jax
import jax.numpy as jnp
import numpy as np
from jax import lax
from jax.experimental import pallas as pl
from jax.experimental.pallas import tpu as pltpu
from jax.sharding import PartitionSpec as P

GROUPS = 32
SIDE = 8
RZ = 4
RY = 4
RX = 4
VOL = SIDE**3
SQ = SIDE * SIDE
NPOS = 16
norm_eps = 1e-05
MESH = pl.DeviceIdType.MESH
BF = jnp.bfloat16
F32 = jnp.float32
VM = pl.BlockSpec(memory_space=pltpu.VMEM)
SM = pl.BlockSpec(memory_space=pltpu.SMEM)


def constants(chans):
    v = np.arange(VOL)
    x, y, z = v % SIDE, v // SIDE % SIDE, v // SQ
    last = SIDE - 1
    masks = np.stack([x < last, x > 0, y < last, y > 0, z < last, z > 0])
    masks = np.broadcast_to(masks[:, None, :], (6, chans, VOL)).astype(np.float32)
    where = (y == 0, y == last, z == 0, z == last)
    spot = (z * SIDE + x, z * SIDE + x, y * SIDE + x, y * SIDE + x)
    sel = np.zeros((4, 2 * VOL, 2 * SQ), np.float32)
    for f in range(4):
        hit = np.nonzero(where[f])[0]
        sel[f, hit, spot[f][hit]] = 1
        sel[f, VOL + hit, SQ + spot[f][hit]] = 1
    half = SIDE // 2
    octant = z // half * 4 + y // half * 2 + x // half
    pool = (octant[None, :] == np.arange(8)[:, None]) / float(half**3)
    lanes = np.arange(8 * chans)
    spread = (np.arange(chans)[:, None] == lanes[None, :] % chans).astype(np.float32)
    octs = (lanes[:, None] // chans == octant[None, :]).astype(np.float32)
    as_bf = lambda a: jnp.asarray(a, BF)
    return as_bf(masks), as_bf(sel), as_bf(pool), as_bf(spread), as_bf(octs)


def silu(x):
    return x * jax.nn.sigmoid(x)


def face_slot(slot_at, face, k):
    a, b = k // 4, k % 4
    if face == 0:
        p = (a * RY + 0) * RX + b
    elif face == 1:
        p = (a * RY + RY - 1) * RX + b
    elif face == 2:
        p = (0 * RY + a) * RX + b
    else:
        p = ((RZ - 1) * RY + a) * RX + b
    return slot_at[p]


def pack_faces(slot_at, ext, sel, faces, stage, chans):
    for f in range(4):
        for k in range(NPOS):
            s = face_slot(slot_at, f, k)
            stage[k // 2 * chans : (k // 2 + 1) * chans, k % 2 * VOL : (k % 2 + 1) * VOL] = ext[s]
        packed = jnp.dot(stage[...], sel[f], preferred_element_type=F32)
        faces[f] = packed.astype(BF)


def unpack_faces(ext, halo, sel, stage, slots, chans):
    for f in range(4):
        wide = lax.dot_general(
            halo[f], sel[f], (((1,), (1,)), ((), ())), preferred_element_type=F32
        ).astype(BF)
        stage[...] = wide
        for k in range(NPOS):
            ext[slots + 1 + f * NPOS + k] = stage[
                k // 2 * chans : (k // 2 + 1) * chans, k % 2 * VOL : (k % 2 + 1) * VOL
            ]


SHIFTS = ((-1, 7), (1, -7), (-8, 56), (8, -56), (-64, 448), (64, -448))


def conv_slot(j, nb, ext, masks, weight):
    own = ext[j]
    taps = [own]
    for d, (a, b) in enumerate(SHIFTS):
        near = ext[nb[d, j]]
        taps.append(
            jnp.where(
                masks[d] > 0.5,
                pltpu.roll(own, a % VOL, 1),
                pltpu.roll(near, b % VOL, 1),
            )
        )
    return jnp.dot(weight, jnp.concatenate(taps, axis=0), preferred_element_type=F32)


def first_faces(slots, chans, slot_at, feat, sel, sig, faces, ext, stage):
    ext[slots] = jnp.zeros((chans, VOL), BF)

    def step(j, c):
        s = silu(feat[j].astype(F32)).astype(BF)
        ext[j] = s
        sig[j] = s
        return c

    lax.fori_loop(0, slots, step, 0, unroll=2)
    pack_faces(slot_at, ext, sel, faces, stage, chans)


def conv_pool(
    slots, chans, cells, slot_at, nb, feat, sig, halo, sel, masks, weight, pool, spread, down,
    level, coarse, stats, ext, stage, pooled, rows,
):
    ext[0:slots] = sig[...]
    ext[slots] = jnp.zeros((chans, VOL), BF)
    unpack_faces(ext, halo, sel, stage, slots, chans)
    pooled[slots] = jnp.zeros((8, chans), F32)
    w = weight[...]
    pm = pool[...]

    def step(j, c):
        f = (feat[j].astype(F32) + conv_slot(j, nb, ext, masks, w)).astype(BF)
        level[j] = f
        pooled[j] = lax.dot_general(pm, f, (((1,), (1,)), ((), ())), preferred_element_type=F32)
        return c

    lax.fori_loop(0, slots, step, 0, unroll=2)
    for p in range(8):
        for q in range(cells):
            z = q // 4 * 2 + p // 4
            x = q // 2 % 2 * 2 + p % 2
            y = q % 2 * 2 + p // 2 % 2
            i = p * cells + q
            rows[i * 8 : (i + 1) * 8, :] = pooled[slot_at[(z * RY + y) * RX + x]]
    wide = jnp.dot(rows[...].astype(BF), spread[...], preferred_element_type=F32)
    n = 8 * cells
    width = 8 * chans
    oct_row = lax.broadcasted_iota(jnp.int32, (n * 8, width), 0) % 8
    oct_lane = lax.broadcasted_iota(jnp.int32, (n * 8, width), 1) // chans
    wide = jnp.where(oct_row == oct_lane, wide, 0.0)
    flat = jnp.sum(wide.reshape(n, 8, width), axis=1).astype(BF)
    acc = jnp.zeros(coarse.shape, F32)
    for p in range(8):
        acc = acc + jnp.dot(
            flat[p * cells : (p + 1) * cells],
            down[p * width : (p + 1) * width, :],
            preferred_element_type=F32,
        )
    coarse[...] = acc
    stats[0:1, :] = jnp.sum(acc, axis=0, keepdims=True)
    stats[1:2, :] = jnp.sum(acc * acc, axis=0, keepdims=True)


def coarse_part(n_my, total, stats, window, gain, bias, weight, part, pad):
    n_mx = lax.axis_size("mx")
    mx = lax.axis_index("mx")
    width = gain.shape[1]
    group = width // GROUPS
    sums = jnp.sum(stats[...], axis=0)
    same = (
        lax.broadcasted_iota(jnp.int32, (width, width), 0) // group
        == lax.broadcasted_iota(jnp.int32, (width, width), 1) // group
    ).astype(F32)
    sums = jnp.concatenate([sums, jnp.zeros((6, width), F32)], axis=0)
    sums = jnp.dot(sums, same, precision=lax.Precision.HIGHEST, preferred_element_type=F32) / total
    mean = sums[0:1]
    std = jnp.sqrt(sums[1:2] - mean * mean + norm_eps)
    g = gain[...]
    b = bias[...]
    pad[...] = jnp.zeros_like(pad)
    for zw in range(4):
        for x in range(2):
            for j in range(n_my):
                value = silu((window[j, zw, x] - mean) / std * g + b)
                if zw == 0:
                    value = jnp.where(mx > 0, value, 0.0)
                if zw == 3:
                    value = jnp.where(mx < n_mx - 1, value, 0.0)
                pad[1 + x, zw, 1 + 2 * j : 3 + 2 * j, :] = value
    tall = 2 * n_my
    acc = jnp.zeros((4 * tall, part.shape[2]), F32)
    t = 0
    for dz in range(3):
        for dy in range(3):
            for dx in range(3):
                lhs = jnp.concatenate(
                    [pad[x + dx, z + dz, dy : dy + tall, :] for z in range(2) for x in range(2)],
                    axis=0,
                ).astype(BF)
                acc = acc + jnp.dot(
                    lhs, weight[t * width : (t + 1) * width, :], preferred_element_type=F32
                )
                t += 1
    for j in range(n_my):
        for zx in range(4):
            part[j, 2 * zx : 2 * zx + 2, :] = acc[zx * tall + 2 * j : zx * tall + 2 * j + 2, :]


def lift_join(
    slots, chans, cells, n_my, slot_at, tgt, result, coarse, up, level, octs, sel,
    out, joined, sig, faces, ext, stage, lifted,
):
    ext[slots] = jnp.zeros((chans, VOL), BF)
    conv = jnp.concatenate([result[j] for j in range(n_my)], axis=1)
    co = (conv + coarse[...]).astype(BF)
    cof = co.astype(F32)
    for q in range(cells):
        z, x, y = q // 4, q // 2 % 2, q % 2
        out[(z * 2 + y) * 2 + x : (z * 2 + y) * 2 + x + 1, :] = cof[q : q + 1]
    width = 8 * chans
    wide = jnp.dot(co, up[...], preferred_element_type=F32)
    for p in range(8):
        lifted[p * cells : (p + 1) * cells, :] = wide[:, p * width : (p + 1) * width]
    pick = (
        lax.broadcasted_iota(jnp.int32, (chans, width), 0)
        == lax.broadcasted_iota(jnp.int32, (chans, width), 1) % chans
    )
    oc = octs[...]

    def step(j, c):
        row = jnp.where(pick, lifted[pl.ds(tgt[j], 1), :], 0.0)
        hi = row.astype(BF)
        lo = (row - hi.astype(F32)).astype(BF)
        both = jnp.dot(jnp.concatenate([hi, lo], axis=0), oc, preferred_element_type=F32)
        f = (level[j].astype(F32) + (both[:chans] + both[chans:])).astype(BF)
        joined[j] = f
        s = silu(f.astype(F32)).astype(BF)
        ext[j] = s
        sig[j] = s
        return c

    lax.fori_loop(0, slots, step, 0, unroll=2)
    pack_faces(slot_at, ext, sel, faces, stage, chans)


def conv_faces(
    slots, chans, slot_at, nb, base, sig, halo, sel, masks, weight,
    level, sig2, faces, ext, ext2, stage,
):
    ext[0:slots] = sig[...]
    ext[slots] = jnp.zeros((chans, VOL), BF)
    ext2[slots] = jnp.zeros((chans, VOL), BF)
    unpack_faces(ext, halo, sel, stage, slots, chans)
    w = weight[...]

    def step(j, c):
        f = (base[j].astype(F32) + conv_slot(j, nb, ext, masks, w)).astype(BF)
        level[j] = f
        s = silu(f.astype(F32)).astype(BF)
        ext2[j] = s
        sig2[j] = s
        return c

    lax.fori_loop(0, slots, step, 0, unroll=2)
    pack_faces(slot_at, ext2, sel, faces, stage, chans)


def conv_last(
    slots, chans, counts, nb, base, sig, halo, sel, masks, weight, out, ext, stage
):
    ext[0:slots] = sig[...]
    ext[slots] = jnp.zeros((chans, VOL), BF)
    unpack_faces(ext, halo, sel, stage, slots, chans)
    w = weight[...]
    n = counts[0]

    def step(j, c):
        f = base[j].astype(F32) + conv_slot(j, nb, ext, masks, w)
        out[j] = jnp.where(j < n, f, 0.0).astype(BF)
        return c

    lax.fori_loop(0, slots, step, 0, unroll=2)


def halo_kernel(faces, halo, send, recv):
    n_mx, n_my = lax.axis_size("mx"), lax.axis_size("my")
    mx, my = lax.axis_index("mx"), lax.axis_index("my")
    peers = (
        (my > 0, mx, my - 1),
        (my < n_my - 1, mx, my + 1),
        (mx > 0, mx - 1, my),
        (mx < n_mx - 1, mx + 1, my),
    )
    barrier = pltpu.get_barrier_semaphore()
    for has, a, b in peers:
        @pl.when(has)
        def _():
            pl.semaphore_signal(barrier, inc=1, device_id=(a, b), device_id_type=MESH)
    pl.semaphore_wait(barrier, sum(jnp.where(has, 1, 0) for has, _, _ in peers))

    def copy(f):
        has, a, b = peers[f]
        return pltpu.make_async_remote_copy(
            src_ref=faces.at[f], dst_ref=halo.at[f], send_sem=send.at[f], recv_sem=recv.at[f],
            device_id=(a, b), device_id_type=MESH,
        )

    for f in range(4):
        @pl.when(peers[f][0])
        def _():
            copy(f).start()

        @pl.when(jnp.logical_not(peers[f ^ 1][0]))
        def _():
            halo[f] = jnp.zeros_like(halo[f])
    for f in range(4):
        @pl.when(peers[f][0])
        def _():
            copy(f).wait_send()

        @pl.when(peers[f ^ 1][0])
        def _():
            copy(f).wait_recv()


def gather_kernel(coarse, stats, window, everyone, send, recv, wsend, wrecv):
    n_mx, n_my = lax.axis_size("mx"), lax.axis_size("my")
    mx, my = lax.axis_index("mx"), lax.axis_index("my")
    n = n_mx * n_my
    me = mx * n_my + my
    barrier = pltpu.get_barrier_semaphore()

    def greet(d, c):
        t = lax.rem(me + d, n)
        pl.semaphore_signal(
            barrier, inc=1, device_id=(t // n_my, lax.rem(t, n_my)), device_id_type=MESH
        )
        return c

    lax.fori_loop(1, n, greet, 0)
    pl.semaphore_wait(barrier, n - 1)

    def stat_copy(d):
        t = lax.rem(me + d, n)
        return pltpu.make_async_remote_copy(
            src_ref=stats, dst_ref=everyone.at[me], send_sem=send.at[d], recv_sem=recv.at[d],
            device_id=(t // n_my, lax.rem(t, n_my)), device_id_type=MESH,
        )

    def go(d, c):
        stat_copy(d).start()
        return c

    def wait(d, c):
        stat_copy(d).wait()
        return c

    def win_copy(kind, d):
        t = lax.rem(my + d, n_my)
        if kind == 0:
            src, dst, a = coarse, window.at[my, pl.ds(1, 2)], mx
        elif kind == 1:
            src, dst, a = coarse.at[pl.ds(0, 1)], window.at[my, pl.ds(3, 1)], mx - 1
        else:
            src, dst, a = coarse.at[pl.ds(1, 1)], window.at[my, pl.ds(0, 1)], mx + 1
        return pltpu.make_async_remote_copy(
            src_ref=src, dst_ref=dst, send_sem=wsend.at[kind, d], recv_sem=wrecv.at[kind, d],
            device_id=(a, t), device_id_type=MESH,
        )

    low, high = mx > 0, mx < n_mx - 1
    for d in range(n_my):
        if d:
            win_copy(0, d).start()

        @pl.when(low)
        def _():
            win_copy(1, d).start()

        @pl.when(high)
        def _():
            win_copy(2, d).start()
    lax.fori_loop(1, n, go, 0)
    window[my, 1:3] = coarse[...]
    everyone[me] = stats[...]

    @pl.when(jnp.logical_not(low))
    def _():
        for j in range(n_my):
            window[j, 0] = jnp.zeros_like(window[j, 0])

    @pl.when(jnp.logical_not(high))
    def _():
        for j in range(n_my):
            window[j, 3] = jnp.zeros_like(window[j, 3])

    for d in range(n_my):
        if d:
            win_copy(0, d).wait()

        @pl.when(low)
        def _():
            win_copy(1, d).wait_send()
            win_copy(2, d).wait_recv()

        @pl.when(high)
        def _():
            win_copy(2, d).wait_send()
            win_copy(1, d).wait_recv()
    lax.fori_loop(1, n, wait, 0)


def result_kernel(part, result, send, recv):
    n_my = lax.axis_size("my")
    mx, my = lax.axis_index("mx"), lax.axis_index("my")
    barrier = pltpu.get_barrier_semaphore()
    for d in range(1, n_my):
        pl.semaphore_signal(
            barrier, inc=1, device_id=(mx, lax.rem(my + d, n_my)), device_id_type=MESH
        )
    pl.semaphore_wait(barrier, n_my - 1)
    copies = []
    for d in range(1, n_my):
        t = lax.rem(my + d, n_my)
        copies.append(
            pltpu.make_async_remote_copy(
                src_ref=part.at[t], dst_ref=result.at[my], send_sem=send.at[d],
                recv_sem=recv.at[d], device_id=(mx, t), device_id_type=MESH,
            )
        )
    for c in copies:
        c.start()
    result[my] = part[my]
    for c in copies:
        c.wait()


def call(fn, out, scratch, n_smem, n_vmem, cid=None):
    params = {} if cid is None else {"collective_id": cid, "has_side_effects": True}
    return pl.pallas_call(
        fn,
        out_shape=out,
        in_specs=[SM] * n_smem + [VM] * n_vmem,
        out_specs=jax.tree.map(lambda _: VM, out),
        scratch_shapes=scratch,
        compiler_params=pltpu.CompilerParams(**params),
    )


def local(
    features, coords, counts, neighbours, fine_weights, down_weight, up_weight, norm_gain,
    norm_bias, coarse_weight,
):
    slots, chans, _ = features.shape
    n_mx, n_my = lax.axis_size("mx"), lax.axis_size("my")
    major, minor = lax.axis_index("mx"), lax.axis_index("my")
    cells = (RZ // 2) * (RY // 2) * (RX // 2)
    width = down_weight.shape[1]
    masks, sel, pool, spread, octs = constants(chans)
    first_slot = (major * n_my + minor) * slots
    live = jnp.arange(slots, dtype=jnp.int32) < counts[0]
    lz = coords[0] - major * RZ
    ly = coords[1] - minor * RY
    lx = coords[2]
    lin = jnp.where(live, (lz * RY + ly) * RX + lx, -1)
    hit = lin[None, :] == jnp.arange(RZ * RY * RX, dtype=jnp.int32)[:, None]
    ids = jnp.arange(slots, dtype=jnp.int32)
    slot_at = slots + jnp.sum(jnp.where(hit, ids - slots, 0), axis=1)
    here = neighbours - first_slot
    spots = jnp.stack([lz * RX + lx] * 4 + [ly * RX + lx] * 2)
    spots = spots + jnp.maximum(jnp.arange(6, dtype=jnp.int32) - 2, 0)[:, None] * NPOS + slots + 1
    nb = jnp.where(here < 0, spots, jnp.where(here >= slots, spots, here))
    nb = jnp.where(neighbours < 0, slots, nb)
    q = (lz // 2 * 2 + lx // 2) * 2 + ly // 2
    p = lz % 2 * 4 + ly % 2 * 2 + lx % 2
    tgt = jnp.where(live, p * cells + q, 0)

    sds = jax.ShapeDtypeStruct
    block = sds((slots, chans, VOL), BF)
    face = sds((4, NPOS // 2 * chans, 2 * SQ), BF)
    ext_rows = slots + 1 + 4 * NPOS
    ext = pltpu.VMEM((ext_rows, chans, VOL), BF)
    ext_small = pltpu.VMEM((slots + 1, chans, VOL), BF)
    stage = pltpu.VMEM((NPOS // 2 * chans, 2 * VOL), BF)
    dma = pltpu.SemaphoreType.DMA

    def exchange(faces, cid):
        return call(halo_kernel, face, [dma((4,)), dma((4,))], 0, 1, cid)(faces)

    sig, faces = call(
        functools.partial(first_faces, slots, chans), (block, face), [ext_small, stage], 1, 2
    )(slot_at, features, sel)
    halo = exchange(faces, 0)
    level, coarse, stats = call(
        functools.partial(conv_pool, slots, chans, cells),
        (block, sds((cells, width), F32), sds((2, width), F32)),
        [ext, stage, pltpu.VMEM((slots + 1, 8, chans), F32),
         pltpu.VMEM((8 * cells * 8, chans), F32)],
        2, 9,
    )(slot_at, nb, features, sig, halo, sel, masks, fine_weights[0], pool, spread, down_weight)
    n = n_mx * n_my
    window, everyone = call(
        gather_kernel,
        (sds((n_my, 4, 2, 2, width), F32), sds((n, 2, width), F32)),
        [dma((n,)), dma((n,)), dma((3, n_my)), dma((3, n_my))],
        0, 2, 1,
    )(coarse.reshape(2, 2, 2, width), stats)
    entries = float(cells * (width // GROUPS) * n)
    part = call(
        functools.partial(coarse_part, n_my, entries),
        sds((n_my, cells, coarse_weight.shape[1]), F32),
        [pltpu.VMEM((4, 4, -(-(2 * n_my + 2) // 8) * 8, width), F32)],
        0, 5,
    )(everyone, window, norm_gain[None, :], norm_bias[None, :], coarse_weight)
    result = call(
        result_kernel, sds(part.shape, F32), [dma((n_my,)), dma((n_my,))], 0, 1, 2
    )(part)
    out, joined, sig, faces = call(
        functools.partial(lift_join, slots, chans, cells, n_my),
        (sds((cells, width), F32), block, block, face),
        [ext_small, stage, pltpu.VMEM((8 * cells, 8 * chans), F32)],
        2, 6,
    )(slot_at, tgt, result, coarse, up_weight, level, octs, sel)
    halo = exchange(faces, 3)
    level, sig, faces = call(
        functools.partial(conv_faces, slots, chans),
        (block, block, face),
        [ext, ext_small, stage],
        2, 6,
    )(slot_at, nb, joined, sig, halo, sel, masks, fine_weights[1])
    halo = exchange(faces, 4)
    fine = call(
        functools.partial(conv_last, slots, chans), block, [ext, stage], 2, 6
    )(counts, nb, level, sig, halo, sel, masks, fine_weights[2])
    return fine, out.astype(BF).reshape(RZ // 2, RY // 2, RX // 2, width)


def solution(mesh):
    in_specs = (
        P(("mx", "my"), None, None),
        P(None, ("mx", "my")),
        P(("mx", "my")),
        P(None, ("mx", "my")),
        P(),
        P(),
        P(),
        P(),
        P(),
        P(None, "my"),
    )
    out_specs = (P(("mx", "my"), None, None), P("mx", "my", None, None))
    return jax.shard_map(local, mesh=mesh, in_specs=in_specs, out_specs=out_specs, check_vma=False)
```

time: 602 us -> 101 us (0.17)
  the two profiles are of different devices: /device:TPU:3 before, /device:TPU:0 now
where the time goes in v1:
time: 101 us; the launch traced here: 100 us
  Pallas kernels  89.1 us (88%)
  local copies, waits for them, and re-layouts  4.97 us (5%)
  other arithmetic  4.96 us (5%)
  between operations  1.35 us (1%)
    pallas_call x3, Pallas kernels, exchange(): return call(halo_kernel, face, [dma((4,)), dma((4,))], 0, 1, cid)(faces)  23.6 us
    pallas_call x1, Pallas kernels, local(): call(functools.partial(conv_pool, slots, chans, cells), (block, sds((cell...  13.3 us
    pallas_call x1, Pallas kernels, local(): call(functools.partial(conv_faces, slots, chans), (block, block, face), [...  10.9 us
    pallas_call x1, Pallas kernels, local(): call(gather_kernel, (sds((n_my, 4, 2, 2, width), F32), sds((n, 2, width),...  10.8 us
    pallas_call x1, Pallas kernels, local(): call(functools.partial(conv_last, slots, chans), block, [ext, stage], 2, 6)  9.93 us
    pallas_call x1, Pallas kernels, local(): call(functools.partial(lift_join, slots, chans, cells, n_my), (sds((cells...  7.92 us
    pallas_call x1, Pallas kernels, local(): call(result_kernel, sds(part.shape, F32), [dma((n_my,)), dma((n_my,))], 0...  5.94 us
    pallas_call x1, Pallas kernels, local(): call(functools.partial(first_faces, slots, chans), (block, face), [ext_sm...  3.55 us

profile of v1, /device:TPU:0, one launch (start us, length us, event | category | flops | bytes accessed | tf_op | source)
XLA Modules:
  0.0 100.3 jit_solution(3549363955386631130)
XLA Ops:
  1.3 1.4 %compare_select_fusion.1.tgt = s32[32]{0:T(128)} fusion(s32[]{:T(128)} %bitcast.51, s32[3,32]{1,0:T(4,128)} %param.16, s32[]{:T(128)S(6)} %mul.50, s32[]{:T(128)S(6)} %mul.53), kind=kLoop, calls=%fused_computation.14 | loop fusion | flops 2272 | bytes 524 | tf_op jit(solution)/shard_map/jit(_where)/select_n | solution.py:475
  2.7 0.8 fusion.3
  3.5 0.1 select_reduce_fusion
  3.6 0.6 broadcast_add_fusion.slot_at
  4.2 1.4 %fusion.1.nb = s32[6,32]{1,0:T(8,128)} fusion(s32[6,32]{1,0:T(8,128)S(1)} %stack.2, s32[6,32]{1,0:T(8,128)} %param.18, s32[6]{0:T(128)S(1)} %maximum_multiply_fusion, s32[]{:T(128)S(6)} %mul.51), kind=kLoop, calls=%fused_computation.7 | loop fusion | flops 1728 | bytes 2332 | tf_op jit(solution)/shard_map/jit(_where)/select_n | solution.py:472
  5.6 1.4 %slice_bitcast_fusion = (bf16[32,224]{1,0:T(8,128)(2,1)}, bf16[32,224]{1,0:T(8,128)(2,1)}, bf16[32,224]{1,0:T(8,128)(2,1)}) fusion(bf16[3,32,224]{2,1,0:T(8,128)(2,1)} %param.19), kind=kLoop, calls=%fused_computation | loop fusion | bytes 86016 | tf_op jit(solution)/shard_map/squeeze | solution.py:533
  6.9 3.5 %shard_map.158 = (bf16[32,32,512]{2,1,0:T(8,128)(2,1)}, bf16[4,256,128]{2,1,0:T(8,128)(2,1)}) custom-call(s32[64]{0:T(128)} %broadcast_add_fusion.slot_at, bf16[32,32,512]{2,1,0:T(8,128)(2,1)} %feat.3, bf16[4,1024,128]{2,1,0:T(8,128)(2,1)} %constant.95.clone.sel), custom_call_target="tpu_custom_call" | custom-call | tf_op jit(solution)/shard_map/pallas_call | solution.py:489
  10.5 9.1 %shard_map.159.halo = bf16[4,256,128]{2,1,0:T(8,128)(2,1)} custom-call(bf16[4,256,128]{2,1,0:T(8,128)(2,1)} %get-tuple-element.17.faces), custom_call_target="tpu_custom_call" | custom-call | tf_op jit(solution)/shard_map/pallas_call | solution.py:487
  19.6 0.0 copy-start
  19.6 13.3 %shard_map.160 = (bf16[32,32,512]{2,1,0:T(8,128)(2,1)}, f32[8,256]{1,0:T(8,128)}, f32[2,256]{1,0:T(2,128)}) custom-call(s32[64]{0:T(128)} %broadcast_add_fusion.slot_at, s32[6,32]{1,0:T(8,128)} %fusion.1.nb, bf16[32,32,512]{2,1,0:T(8,128)(2,1)} %feat.3, bf16[32,32,512]{2,1,0:T(8,128)(2,1)} %get-tuple-element.16.sig, bf16[4,256,128]{2,1,0:T(8,128)(2,1)} %shard_map.159.halo, ...), custom_call_target="tpu_custom_call" | custom-call | tf_op jit(solution)/shard_map/pallas_call | solution.py:493
  33.0 1.3 %reshape.28.coarse = f32[2,2,2,256]{3,2,1,0:T(2,128)} reshape(f32[8,256]{1,0:T(8,128)} %get-tuple-element.18.coarse) | data formatting | bytes 16384 | tf_op jit(solution)/shard_map/reshape | solution.py:506
  34.3 10.8 %shard_map.161 = (f32[4,4,2,2,256]{4,3,2,1,0:T(2,128)}, f32[32,2,256]{2,1,0:T(2,128)}) custom-call(f32[2,2,2,256]{3,2,1,0:T(2,128)} %reshape.28.coarse, f32[2,256]{1,0:T(2,128)} %get-tuple-element.19.stats), custom_call_target="tpu_custom_call" | custom-call | tf_op jit(solution)/shard_map/pallas_call | solution.py:501
  45.1 0.0 copy-done
  45.1 1.7 %copy.18.weight = bf16[6912,64]{1,0:T(8,128)(2,1)} copy(bf16[6912,64]{0,1:T(8,128)(2,1)S(1)} %copy-done) | data formatting | bytes 1769472 | tf_op args[9]
  46.8 3.1 %shard_map.162.part = f32[4,8,64]{2,1,0:T(8,128)} custom-call(f32[32,2,256]{2,1,0:T(2,128)} %get-tuple-element.20.stats, f32[4,4,2,2,256]{4,3,2,1,0:T(2,128)} %get-tuple-element.21.window, f32[1,256]{1,0:T(1,128)} %bitcast.52, f32[1,256]{1,0:T(1,128)} %bitcast.53, bf16[6912,64]{1,0:T(8,128)(2,1)} %copy.18.weight), custom_call_target="tpu_custom_call" | custom-call | tf_op jit(solution)/shard_map/pallas_call | solution.py:508
  49.9 5.9 %shard_map.163.result = f32[4,8,64]{2,1,0:T(8,128)} custom-call(f32[4,8,64]{2,1,0:T(8,128)} %shard_map.162.part), custom_call_target="tpu_custom_call" | custom-call | tf_op jit(solution)/shard_map/pallas_call | solution.py:514
  55.8 7.9 %shard_map.164 = (f32[8,256]{1,0:T(8,128)}, bf16[32,32,512]{2,1,0:T(8,128)(2,1)}, bf16[32,32,512]{2,1,0:T(8,128)(2,1)}, bf16[4,256,128]{2,1,0:T(8,128)(2,1)}) custom-call(s32[64]{0:T(128)} %broadcast_add_fusion.slot_at, s32[32]{0:T(128)} %compare_select_fusion.1.tgt, f32[4,8,64]{2,1,0:T(8,128)} %shard_map.163.result, f32[8,256]{1,0:T(8,128)} %get-tuple-element.18.coarse, ...), custom_call_target="tpu_custom_call" | custom-call | tf_op jit(solution)/shard_map/pallas_call | solution.py:517
  63.7 0.7 convert_element_type.3
  64.4 0.6 reshape.29
  65.0 6.8 %shard_map.165.halo = bf16[4,256,128]{2,1,0:T(8,128)(2,1)} custom-call(bf16[4,256,128]{2,1,0:T(8,128)(2,1)} %get-tuple-element.25.faces), custom_call_target="tpu_custom_call" | custom-call | tf_op jit(solution)/shard_map/pallas_call | solution.py:487
  71.9 10.9 %shard_map.166 = (bf16[32,32,512]{2,1,0:T(8,128)(2,1)}, bf16[32,32,512]{2,1,0:T(8,128)(2,1)}, bf16[4,256,128]{2,1,0:T(8,128)(2,1)}) custom-call(s32[64]{0:T(128)} %broadcast_add_fusion.slot_at, s32[6,32]{1,0:T(8,128)} %fusion.1.nb, bf16[32,32,512]{2,1,0:T(8,128)(2,1)} %get-tuple-element.23.base, bf16[32,32,512]{2,1,0:T(8,128)(2,1)} %get-tuple-element.24.sig, ...), custom_call_target="tpu_custom_call" | custom-call | tf_op jit(solution)/shard_map/pallas_call | solution.py:524
  82.8 7.6 %shard_map.167.halo = bf16[4,256,128]{2,1,0:T(8,128)(2,1)} custom-call(bf16[4,256,128]{2,1,0:T(8,128)(2,1)} %get-tuple-element.28.faces), custom_call_target="tpu_custom_call" | custom-call | tf_op jit(solution)/shard_map/pallas_call | solution.py:487
  90.4 9.9 %shard_map.168 = bf16[32,32,512]{2,1,0:T(8,128)(2,1)} custom-call(s32[1]{0:T(128)} %copy.19.counts, s32[6,32]{1,0:T(8,128)} %fusion.1.nb, bf16[32,32,512]{2,1,0:T(8,128)(2,1)} %get-tuple-element.26.base, bf16[32,32,512]{2,1,0:T(8,128)(2,1)} %get-tuple-element.27.sig, bf16[4,256,128]{2,1,0:T(8,128)(2,1)} %shard_map.167.halo, ...), custom_call_target="tpu_custom_call" | custom-call | tf_op jit(solution)/shard_map/pallas_call | solution.py:531
  (3 shorter events, 0.0 us)
Async XLA Ops:
  19.6 25.5 %copy-start = (bf16[6912,64]{0,1:T(8,128)(2,1)S(1)}, bf16[6912,64]{0,1:T(8,128)(2,1)}, u32[]{:S(2)}) copy-start(bf16[6912,64]{0,1:T(8,128)(2,1)} %param.24) | copy-start | bytes 2654212

commit v2 on v1

v2 whole, which is shorter than its diff:
```python
import functools

import jax
import jax.numpy as jnp
import numpy as np
from jax import lax
from jax.experimental import pallas as pl
from jax.experimental.pallas import tpu as pltpu
from jax.sharding import PartitionSpec as P

GROUPS = 32
SIDE = 8
RZ = 4
RY = 4
RX = 4
VOL = SIDE**3
SQ = SIDE * SIDE
NPOS = 16
norm_eps = 1e-05
MESH = pl.DeviceIdType.MESH
BF = jnp.bfloat16
F32 = jnp.float32
VM = pl.BlockSpec(memory_space=pltpu.VMEM)
SM = pl.BlockSpec(memory_space=pltpu.SMEM)


def constants(chans):
    v = np.arange(VOL)
    x, y, z = v % SIDE, v // SIDE % SIDE, v // SQ
    last = SIDE - 1
    masks = np.stack([x < last, x > 0, y < last, y > 0, z < last, z > 0])
    masks = np.broadcast_to(masks[:, None, :], (6, chans, VOL)).astype(np.float32)
    where = (y == 0, y == last, z == 0, z == last)
    spot = (z * SIDE + x, z * SIDE + x, y * SIDE + x, y * SIDE + x)
    sel = np.zeros((4, 2 * VOL, 2 * SQ), np.float32)
    for f in range(4):
        hit = np.nonzero(where[f])[0]
        sel[f, hit, spot[f][hit]] = 1
        sel[f, VOL + hit, SQ + spot[f][hit]] = 1
    half = SIDE // 2
    octant = z // half * 4 + y // half * 2 + x // half
    pool = (octant[None, :] == np.arange(8)[:, None]) / float(half**3)
    lanes = np.arange(8 * chans)
    spread = (np.arange(chans)[:, None] == lanes[None, :] % chans).astype(np.float32)
    octs = (lanes[:, None] // chans == octant[None, :]).astype(np.float32)
    as_bf = lambda a: jnp.asarray(a, BF)
    return as_bf(masks), as_bf(sel), as_bf(pool), as_bf(spread), as_bf(octs)


def silu(x):
    return x * jax.nn.sigmoid(x)


def face_slot(slot_at, face, k):
    a, b = k // 4, k % 4
    if face == 0:
        p = (a * RY + 0) * RX + b
    elif face == 1:
        p = (a * RY + RY - 1) * RX + b
    elif face == 2:
        p = (0 * RY + a) * RX + b
    else:
        p = ((RZ - 1) * RY + a) * RX + b
    return slot_at[p]


SHIFTS = ((-1, 7), (1, -7), (-8, 56), (8, -56), (-64, 448), (64, -448))


def tap(d, own, near, masks):
    a, b = SHIFTS[d]
    return jnp.where(masks[d] > 0.5, pltpu.roll(own, a % VOL, 1), pltpu.roll(near, b % VOL, 1))


def level_kernel(
    slots, chans, cells,
    slot_at, coords, counts, neighbours,
    feat, fine_w, gain, bias, pool, spread,
    masks_h, sel_h, octs_h, down_h, up_h, weight_h,
    out, coarse_out,
    masks, sel, octs, down, up, weight,
    ext, ext2, acc, level, stage, faces, halo, pooled, rows, coarse, stats,
    window, everyone, pad, part, result, lifted, nb, tgt,
    load, fsend, frecv, ssend, srecv, wsend, wrecv, rsend, rrecv,
):
    n_mx, n_my = lax.axis_size("mx"), lax.axis_size("my")
    mx, my = lax.axis_index("mx"), lax.axis_index("my")
    n = n_mx * n_my
    me = mx * n_my + my
    width = 8 * chans
    wide_c = gain.shape[1]

    loads = [
        pltpu.make_async_copy(a, b, load.at[i])
        for i, (a, b) in enumerate(
            ((sel_h, sel), (masks_h, masks), (down_h, down), (weight_h, weight),
             (up_h, up), (octs_h, octs))
        )
    ]
    for c in loads:
        c.start()

    barrier = pltpu.get_barrier_semaphore()

    def where_is(d):
        t = lax.rem(me + d, n)
        return (t // n_my, lax.rem(t, n_my))

    def greet(d, c):
        pl.semaphore_signal(barrier, inc=1, device_id=where_is(d), device_id_type=MESH)
        return c

    lax.fori_loop(1, n, greet, 0)

    ext[slots] = jnp.zeros((chans, VOL), BF)
    ext2[slots] = jnp.zeros((chans, VOL), BF)
    first_slot = me * slots
    count = counts[0]

    def begin(j, c):
        s = silu(feat[j].astype(F32)).astype(BF)
        ext[j] = s
        z = coords[0, j] - mx * RZ
        y = coords[1, j] - my * RY
        x = coords[2, j]
        for d in range(6):
            g = neighbours[d, j]
            here = g - first_slot
            spot = jnp.clip((z if d < 4 else y) * RX + x, 0, NPOS - 1)
            far = slots + 1 + max(d - 2, 0) * NPOS + spot
            inside = (here >= 0) & (here < slots)
            nb[d, j] = jnp.where(g < 0, slots, jnp.where(inside, here, far))
        q = (z // 2 * 2 + x // 2) * 2 + y // 2
        p = z % 2 * 4 + y % 2 * 2 + x % 2
        tgt[j] = jnp.clip(jnp.where(j < count, p * cells + q, 0), 0, 8 * cells - 1)
        return c

    lax.fori_loop(0, slots, begin, 0, unroll=2)
    loads[0].wait()

    peers = (
        (my > 0, mx, my - 1),
        (my < n_my - 1, mx, my + 1),
        (mx > 0, mx - 1, my),
        (mx < n_mx - 1, mx + 1, my),
    )

    def face_copy(r, f):
        _, a, b = peers[f]
        return pltpu.make_async_remote_copy(
            src_ref=faces.at[r, f], dst_ref=halo.at[r, f], send_sem=fsend.at[r, f],
            recv_sem=frecv.at[r, f], device_id=(a, b), device_id_type=MESH,
        )

    def send_faces(r, src):
        for f in range(4):
            for k in range(NPOS):
                s = face_slot(slot_at, f, k)
                stage[
                    k // 2 * chans : (k // 2 + 1) * chans, k % 2 * VOL : (k % 2 + 1) * VOL
                ] = src[s]
            faces[r, f] = jnp.dot(stage[...], sel[f], preferred_element_type=F32).astype(BF)
            if r == 0 and f == 0:
                pl.semaphore_wait(barrier, n - 1)

            @pl.when(peers[f][0])
            def _():
                face_copy(r, f).start()

            @pl.when(jnp.logical_not(peers[f ^ 1][0]))
            def _():
                halo[r, f] = jnp.zeros_like(halo[r, f])

    def take_faces(r, dst):
        for f in range(4):
            @pl.when(peers[f][0])
            def _():
                face_copy(r, f).wait_send()

            @pl.when(peers[f ^ 1][0])
            def _():
                face_copy(r, f).wait_recv()

            stage[...] = lax.dot_general(
                halo[r, f], sel[f], (((1,), (1,)), ((), ())), preferred_element_type=F32
            ).astype(BF)
            for k in range(NPOS):
                dst[slots + 1 + f * NPOS + k] = stage[
                    k // 2 * chans : (k // 2 + 1) * chans, k % 2 * VOL : (k % 2 + 1) * VOL
                ]

    def conv(r, base, src, finish):
        w = fine_w[r]
        w_near, w_far = w[:, : 3 * chans], w[:, 3 * chans :]

        def near_pass(j, c):
            own = src[j]
            taps = [own] + [tap(d, own, src[nb[d, j]], masks) for d in (0, 1)]
            acc[j] = base[j].astype(F32) + jnp.dot(
                w_near, jnp.concatenate(taps, axis=0), preferred_element_type=F32
            )
            return c

        lax.fori_loop(0, slots, near_pass, 0, unroll=2)
        take_faces(r, src)

        def far_pass(j, c):
            own = src[j]
            taps = [tap(d, own, src[nb[d, j]], masks) for d in (2, 3, 4, 5)]
            finish(
                j,
                acc[j] + jnp.dot(
                    w_far, jnp.concatenate(taps, axis=0), preferred_element_type=F32
                ),
            )
            return c

        lax.fori_loop(0, slots, far_pass, 0, unroll=2)

    send_faces(0, ext)
    loads[1].wait()

    pooled[slots] = jnp.zeros((8, chans), F32)
    pm = pool[...]

    def first_done(j, value):
        f = value.astype(BF)
        level[j] = f
        pooled[j] = lax.dot_general(pm, f, (((1,), (1,)), ((), ())), preferred_element_type=F32)

    conv(0, feat, ext, first_done)
    for p in range(8):
        for q in range(cells):
            z = q // 4 * 2 + p // 4
            x = q // 2 % 2 * 2 + p % 2
            y = q % 2 * 2 + p // 2 % 2
            i = p * cells + q
            rows[i * 8 : (i + 1) * 8, :] = pooled[slot_at[(z * RY + y) * RX + x]]
    wide = jnp.dot(rows[...].astype(BF), spread[...], preferred_element_type=F32)
    m = 8 * cells
    oct_row = lax.broadcasted_iota(jnp.int32, (m * 8, width), 0) % 8
    oct_lane = lax.broadcasted_iota(jnp.int32, (m * 8, width), 1) // chans
    wide = jnp.where(oct_row == oct_lane, wide, 0.0)
    flat = jnp.sum(wide.reshape(m, 8, width), axis=1).astype(BF)
    loads[2].wait()
    ci = jnp.zeros((cells, wide_c), F32)
    for p in range(8):
        ci = ci + jnp.dot(
            flat[p * cells : (p + 1) * cells],
            down[p * width : (p + 1) * width, :],
            preferred_element_type=F32,
        )
    layer = cells // 2
    coarse[0] = ci[:layer]
    coarse[1] = ci[layer:]
    stats[0:1, :] = jnp.sum(ci, axis=0, keepdims=True)
    stats[1:2, :] = jnp.sum(ci * ci, axis=0, keepdims=True)

    def stat_copy(d):
        return pltpu.make_async_remote_copy(
            src_ref=stats, dst_ref=everyone.at[me], send_sem=ssend.at[d], recv_sem=srecv.at[d],
            device_id=where_is(d), device_id_type=MESH,
        )

    def stat_go(d, c):
        stat_copy(d).start()
        return c

    def stat_wait(d, c):
        stat_copy(d).wait()
        return c

    def win_copy(kind, d):
        t = lax.rem(my + d, n_my)
        if kind == 0:
            src, dst, a = coarse, window.at[my, pl.ds(1, 2)], mx
        elif kind == 1:
            src, dst, a = coarse.at[pl.ds(0, 1)], window.at[my, pl.ds(3, 1)], mx - 1
        else:
            src, dst, a = coarse.at[pl.ds(1, 1)], window.at[my, pl.ds(0, 1)], mx + 1
        return pltpu.make_async_remote_copy(
            src_ref=src, dst_ref=dst, send_sem=wsend.at[kind, d], recv_sem=wrecv.at[kind, d],
            device_id=(a, t), device_id_type=MESH,
        )

    lax.fori_loop(1, n, stat_go, 0)
    low, high = mx > 0, mx < n_mx - 1
    for d in range(n_my):
        if d:
            win_copy(0, d).start()

        @pl.when(low)
        def _():
            win_copy(1, d).start()

        @pl.when(high)
        def _():
            win_copy(2, d).start()
    window[my, 1:3] = coarse[...]
    everyone[me] = stats[...]

    @pl.when(jnp.logical_not(low))
    def _():
        for j in range(n_my):
            window[j, 0] = jnp.zeros_like(window[j, 0])

    @pl.when(jnp.logical_not(high))
    def _():
        for j in range(n_my):
            window[j, 3] = jnp.zeros_like(window[j, 3])

    pad[...] = jnp.zeros_like(pad)
    group = wide_c // GROUPS
    same = (
        lax.broadcasted_iota(jnp.int32, (wide_c, wide_c), 0) // group
        == lax.broadcasted_iota(jnp.int32, (wide_c, wide_c), 1) // group
    ).astype(F32)
    for c in loads[3:]:
        c.wait()
    for d in range(n_my):
        if d:
            win_copy(0, d).wait()

        @pl.when(low)
        def _():
            win_copy(1, d).wait_send()
            win_copy(2, d).wait_recv()

        @pl.when(high)
        def _():
            win_copy(2, d).wait_send()
            win_copy(1, d).wait_recv()
    lax.fori_loop(1, n, stat_wait, 0)

    total = float(cells * group) * n
    sums = jnp.sum(everyone[...], axis=0)
    sums = jnp.concatenate([sums, jnp.zeros((6, wide_c), F32)], axis=0)
    sums = jnp.dot(sums, same, precision=lax.Precision.HIGHEST, preferred_element_type=F32) / total
    mean = sums[0:1]
    std = jnp.sqrt(sums[1:2] - mean * mean + norm_eps)
    g = gain[...]
    b = bias[...]
    for zw in range(4):
        for j in range(n_my):
            value = silu((window[j, zw] - mean) / std * g + b)
            if zw == 0:
                value = jnp.where(low, value, 0.0)
            if zw == 3:
                value = jnp.where(high, value, 0.0)
            for x in range(2):
                pad[1 + x, zw, 1 + 2 * j : 3 + 2 * j, :] = value[2 * x : 2 * x + 2]
    tall = 2 * n_my
    sums = jnp.zeros((4 * tall, part.shape[2]), F32)
    t = 0
    for dz in range(3):
        for dy in range(3):
            for dx in range(3):
                lhs = jnp.concatenate(
                    [pad[x + dx, z + dz, dy : dy + tall, :] for z in range(2) for x in range(2)],
                    axis=0,
                ).astype(BF)
                sums = sums + lax.dot_general(
                    lhs, weight[:, t * wide_c : (t + 1) * wide_c], (((1,), (1,)), ((), ())),
                    preferred_element_type=F32,
                )
                t += 1
    for j in range(n_my):
        for zx in range(4):
            part[j, 2 * zx : 2 * zx + 2, :] = sums[zx * tall + 2 * j : zx * tall + 2 * j + 2, :]
    copies = []
    for d in range(1, n_my):
        to = lax.rem(my + d, n_my)
        copies.append(
            pltpu.make_async_remote_copy(
                src_ref=part.at[to], dst_ref=result.at[my], send_sem=rsend.at[d],
                recv_sem=rrecv.at[d], device_id=(mx, to), device_id_type=MESH,
            )
        )
    for c in copies:
        c.start()
    result[my] = part[my]
    for c in copies:
        c.wait()

    whole = jnp.concatenate([result[j] for j in range(n_my)], axis=1)
    co = (whole + jnp.concatenate([coarse[0], coarse[1]], axis=0)).astype(BF)
    cof = co.astype(F32)
    for q in range(cells):
        z, x, y = q // 4, q // 2 % 2, q % 2
        coarse_out[(z * 2 + y) * 2 + x : (z * 2 + y) * 2 + x + 1, :] = cof[q : q + 1]
    wide = jnp.dot(co, up[...], preferred_element_type=F32)
    for p in range(8):
        for q in range(cells):
            lifted[p * cells + q] = wide[q : q + 1, p * width : (p + 1) * width]
    pick = (
        lax.broadcasted_iota(jnp.int32, (chans, width), 0)
        == lax.broadcasted_iota(jnp.int32, (chans, width), 1) % chans
    )
    oc = octs[...]

    def join(j, c):
        row = jnp.where(pick, lifted[tgt[j]], 0.0)
        hi = row.astype(BF)
        lo = (row - hi.astype(F32)).astype(BF)
        both = jnp.dot(jnp.concatenate([hi, lo], axis=0), oc, preferred_element_type=F32)
        f = (level[j].astype(F32) + (both[:chans] + both[chans:])).astype(BF)
        level[j] = f
        ext[j] = silu(f.astype(F32)).astype(BF)
        return c

    lax.fori_loop(0, slots, join, 0, unroll=2)
    send_faces(1, ext)

    def second_done(j, value):
        f = value.astype(BF)
        level[j] = f
        ext2[j] = silu(f.astype(F32)).astype(BF)

    conv(1, level, ext, second_done)
    send_faces(2, ext2)

    def last_done(j, value):
        out[j] = jnp.where(j < count, value, 0.0).astype(BF)

    conv(2, level, ext2, last_done)


def local(
    features, coords, counts, neighbours, fine_weights, down_weight, up_weight, norm_gain,
    norm_bias, coarse_weight,
):
    slots, chans, _ = features.shape
    n_mx, n_my = lax.axis_size("mx"), lax.axis_size("my")
    major, minor = lax.axis_index("mx"), lax.axis_index("my")
    cells = (RZ // 2) * (RY // 2) * (RX // 2)
    width = down_weight.shape[1]
    masks, sel, pool, spread, octs = constants(chans)
    ids = jnp.arange(slots, dtype=jnp.int32)
    lin = ((coords[0] - major * RZ) * RY + coords[1] - minor * RY) * RX + coords[2]
    lin = jnp.where(ids < counts[0], lin, -1)
    hit = lin[None, :] == jnp.arange(RZ * RY * RX, dtype=jnp.int32)[:, None]
    slot_at = slots + jnp.sum(jnp.where(hit, ids - slots, 0), axis=1)
    n = n_mx * n_my
    sds = jax.ShapeDtypeStruct
    weight_t = coarse_weight.T
    held = [
        pltpu.VMEM(a.shape, a.dtype)
        for a in (masks, sel, octs, down_weight, up_weight, weight_t)
    ]
    ext = pltpu.VMEM((slots + 1 + 4 * NPOS, chans, VOL), BF)
    ext_small = pltpu.VMEM((slots, chans, VOL), BF)
    pairs = NPOS // 2 * chans
    dma = pltpu.SemaphoreType.DMA
    scratch = held + [
        ext, ext,
        pltpu.VMEM((slots, chans, VOL), F32),
        ext_small,
        pltpu.VMEM((pairs, 2 * VOL), BF),
        pltpu.VMEM((3, 4, pairs, 2 * SQ), BF),
        pltpu.VMEM((3, 4, pairs, 2 * SQ), BF),
        pltpu.VMEM((slots + 1, 8, chans), F32),
        pltpu.VMEM((8 * cells * 8, chans), F32),
        pltpu.VMEM((2, cells // 2, width), F32),
        pltpu.VMEM((2, width), F32),
        pltpu.VMEM((n_my, 4, cells // 2, width), F32),
        pltpu.VMEM((n, 2, width), F32),
        pltpu.VMEM((4, 4, -(-(2 * n_my + 2) // 8) * 8, width), F32),
        pltpu.VMEM((n_my, cells, coarse_weight.shape[1]), F32),
        pltpu.VMEM((n_my, cells, coarse_weight.shape[1]), F32),
        pltpu.VMEM((8 * cells, 1, 8 * chans), F32),
        pltpu.SMEM((6, slots), jnp.int32),
        pltpu.SMEM((slots,), jnp.int32),
        dma((6,)), dma((3, 4)), dma((3, 4)), dma((n,)), dma((n,)),
        dma((3, n_my)), dma((3, n_my)), dma((n_my,)), dma((n_my,)),
    ]
    fine, out = pl.pallas_call(
        functools.partial(level_kernel, slots, chans, cells),
        out_shape=(sds(features.shape, BF), sds((cells, width), F32)),
        in_specs=[SM] * 4 + [VM] * 6 + [pl.BlockSpec(memory_space=pl.ANY)] * 6,
        out_specs=(VM, VM),
        scratch_shapes=scratch,
        compiler_params=pltpu.CompilerParams(collective_id=0, has_side_effects=True),
    )(
        slot_at, coords, counts, neighbours, features, fine_weights, norm_gain[None, :],
        norm_bias[None, :], pool, spread, masks, sel, octs, down_weight, up_weight, weight_t,
    )
    return fine, out.astype(BF).reshape(RZ // 2, RY // 2, RX // 2, width)


def solution(mesh):
    in_specs = (
        P(("mx", "my"), None, None),
        P(None, ("mx", "my")),
        P(("mx", "my")),
        P(None, ("mx", "my")),
        P(),
        P(),
        P(),
        P(),
        P(),
        P(None, "my"),
    )
    out_specs = (P(("mx", "my"), None, None), P("mx", "my", None, None))
    return jax.shard_map(local, mesh=mesh, in_specs=in_specs, out_specs=out_specs, check_vma=False)
```

time: 101 us -> 67.8 us (0.67)
  Pallas kernels: 89.1 us -> 62 us
  other arithmetic: 4.96 us -> 1.32 us
  local copies, waits for them, and re-layouts: 4.97 us -> 2.93 us
    pallas_call x11 -> x1, Pallas kernels: 89.1 us -> 62 us  [local(): pl.pallas_call(functools.partial(level_kernel, slots, chans, cells), out_...]
    select_n x2 -> x0, other arithmetic: 2.76 us -> none  [the longest x1 1.41 us: local(): tgt = jnp.where(live, p * cells + q, 0)]
    squeeze x1 -> x0, local copies, waits for them, and re-layouts: 1.37 us -> none  [local(): fine_weights[2]]
    reshape x1 -> x0, local copies, waits for them, and re-layouts: 1.3 us -> none  [local(): coarse.reshape(2, 2, 2, width)]
where the time goes in v2:
time: 67.8 us; the launch traced here: 67.6 us
  Pallas kernels  62 us (91%)
  local copies, waits for them, and re-layouts  2.93 us (4%)
  other arithmetic  1.32 us (2%)
  between operations  1.32 us (2%)
    pallas_call x1, Pallas kernels, local(): pl.pallas_call(functools.partial(level_kernel, slots, chans, cells), out_...  62 us
    unnamed x3, local copies, waits for them, and re-layouts  2.32 us

profile of v2, /device:TPU:0, one launch (start us, length us, event | category | flops | bytes accessed | tf_op | source)
XLA Modules:
  0.0 67.6 jit_solution(5495602552780436578)
XLA Ops:
  0.6 0.0 copy-start
  1.3 0.0 copy-done
  1.3 0.1 select_reduce_fusion
  1.4 0.5 broadcast_add_fusion.slot_at
  2.0 62.0 %shard_map.158 = (bf16[32,32,512]{2,1,0:T(8,128)(2,1)}, f32[8,256]{1,0:T(8,128)}) custom-call(s32[64]{0:T(128)} %broadcast_add_fusion.slot_at, s32[3,32]{1,0:T(4,128)} %coords.1, s32[1]{0:T(128)} %copy.18.counts, s32[6,32]{1,0:T(8,128)} %neighbours.1, bf16[32,32,512]{2,1,0:T(8,128)(2,1)} %feat.1, bf16[3,32,224]{2,1,0:T(8,128)(2,1)} %fine_w.1, ...), custom_call_target="tpu_custom_call" | custom-call | tf_op jit(solution)/shard_map/pallas_call | solution.py:476
  64.0 0.7 %convert_element_type.3 = bf16[8,256]{1,0:T(8,128)(2,1)S(1)} convert(f32[8,256]{1,0:T(8,128)} %get-tuple-element.5) | non-fusion elementwise | flops 2048 | bytes 12288 | tf_op jit(solution)/shard_map/convert_element_type | solution.py:487
  64.7 0.6 reshape.14
  65.3 2.3 %copy.19 = bf16[32,32,512]{2,1,0:T(8,128)(2,1)} copy(bf16[32,32,512]{2,1,0:T(8,128)(2,1)} %get-tuple-element.8) | data formatting | bytes 2097152
  (2 shorter events, 0.0 us)
Async XLA Ops:
  0.6 0.7 %copy-start = (s32[3,32]{1,0:T(4,128)S(1)}, s32[3,32]{1,0:T(4,128)}, u32[]{:S(2)}) copy-start(s32[3,32]{1,0:T(4,128)} %coords.1) | copy-start | bytes 1156

commit v3 on v2

--- a/solution.py
+++ b/solution.py
@@ -16,6 +16,8 @@
 VOL = SIDE**3
 SQ = SIDE * SIDE
 NPOS = 16
+LANES = 2 * SQ
+CHUNKS = VOL // LANES
 norm_eps = 1e-05
 MESH = pl.DeviceIdType.MESH
 BF = jnp.bfloat16
@@ -28,23 +30,19 @@
     v = np.arange(VOL)
     x, y, z = v % SIDE, v // SIDE % SIDE, v // SQ
     last = SIDE - 1
-    masks = np.stack([x < last, x > 0, y < last, y > 0, z < last, z > 0])
-    masks = np.broadcast_to(masks[:, None, :], (6, chans, VOL)).astype(np.float32)
-    where = (y == 0, y == last, z == 0, z == last)
-    spot = (z * SIDE + x, z * SIDE + x, y * SIDE + x, y * SIDE + x)
-    sel = np.zeros((4, 2 * VOL, 2 * SQ), np.float32)
-    for f in range(4):
-        hit = np.nonzero(where[f])[0]
-        sel[f, hit, spot[f][hit]] = 1
-        sel[f, VOL + hit, SQ + spot[f][hit]] = 1
+    lane = np.arange(LANES)
+    near = [x < last, x > 0, y < last, y > 0]
+    masks = [m[:LANES] for m in near] + [lane < SQ]
+    masks += [lane // SIDE % SIDE == k for k in range(SIDE)]
+    masks = np.broadcast_to(np.stack(masks)[:, None, :], (5 + SIDE, chans, LANES))
     half = SIDE // 2
     octant = z // half * 4 + y // half * 2 + x // half
     pool = (octant[None, :] == np.arange(8)[:, None]) / float(half**3)
     lanes = np.arange(8 * chans)
     spread = (np.arange(chans)[:, None] == lanes[None, :] % chans).astype(np.float32)
     octs = (lanes[:, None] // chans == octant[None, :]).astype(np.float32)
-    as_bf = lambda a: jnp.asarray(a, BF)
-    return as_bf(masks), as_bf(sel), as_bf(pool), as_bf(spread), as_bf(octs)
+    as_bf = lambda a: jnp.asarray(np.asarray(a, np.float32), BF)
+    return as_bf(masks), as_bf(pool), as_bf(spread), as_bf(octs)
 
 
 def silu(x):
@@ -64,22 +62,40 @@
     return slot_at[p]
 
 
-SHIFTS = ((-1, 7), (1, -7), (-8, 56), (8, -56), (-64, 448), (64, -448))
-
-
-def tap(d, own, near, masks):
-    a, b = SHIFTS[d]
-    return jnp.where(masks[d] > 0.5, pltpu.roll(own, a % VOL, 1), pltpu.roll(near, b % VOL, 1))
+def chunk(ref, row, i):
+    return ref[row, :, i * LANES : (i + 1) * LANES]
+
+
+def turn(value, shift):
+    return pltpu.roll(value, shift % LANES, 1) if shift % LANES else value
+
+
+def side_tap(src, j, row, shift, span, keep):
+    parts = []
+    for i in range(CHUNKS):
+        own = turn(chunk(src, j, i), -shift)
+        near = turn(chunk(src, row, i), shift * (span - 1))
+        parts.append(jnp.where(keep, own, near))
+    return jnp.concatenate(parts, axis=1)
+
+
+def depth_taps(src, j, up, down, low):
+    turned = [turn(chunk(src, down, CHUNKS - 1), SQ)]
+    turned += [turn(chunk(src, j, i), SQ) for i in range(CHUNKS)]
+    turned += [turn(chunk(src, up, 0), SQ)]
+    plus = [jnp.where(low, turned[i + 1], turned[i + 2]) for i in range(CHUNKS)]
+    minus = [jnp.where(low, turned[i], turned[i + 1]) for i in range(CHUNKS)]
+    return jnp.concatenate(plus, axis=1), jnp.concatenate(minus, axis=1)
 
 
 def level_kernel(
     slots, chans, cells,
     slot_at, coords, counts, neighbours,
-    feat, fine_w, gain, bias, pool, spread,
-    masks_h, sel_h, octs_h, down_h, up_h, weight_h,
+    feat, fine_w, gain, bias, pool, spread, masks,
+    octs_h, down_h, up_h, weight_h,
     out, coarse_out,
-    masks, sel, octs, down, up, weight,
-    ext, ext2, acc, level, stage, faces, halo, pooled, rows, coarse, stats,
+    octs, down, up, weight,
+    ext, ext2, acc, level, faces, halo, pooled, rows, coarse, stats,
     window, everyone, pad, part, result, lifted, nb, tgt,
     load, fsend, frecv, ssend, srecv, wsend, wrecv, rsend, rrecv,
 ):
@@ -93,7 +109,7 @@
     loads = [
         pltpu.make_async_copy(a, b, load.at[i])
         for i, (a, b) in enumerate(
-            ((sel_h, sel), (masks_h, masks), (down_h, down), (weight_h, weight),
+            ((down_h, down), (weight_h, weight),
              (up_h, up), (octs_h, octs))
         )
     ]
@@ -136,7 +152,8 @@
         return c
 
     lax.fori_loop(0, slots, begin, 0, unroll=2)
-    loads[0].wait()
+    keep = [masks[i] > 0.5 for i in range(5)]
+    low_half = keep[4]
 
     peers = (
         (my > 0, mx, my - 1),
@@ -154,12 +171,25 @@
 
     def send_faces(r, src):
         for f in range(4):
-            for k in range(NPOS):
-                s = face_slot(slot_at, f, k)
-                stage[
-                    k // 2 * chans : (k // 2 + 1) * chans, k % 2 * VOL : (k % 2 + 1) * VOL
-                ] = src[s]
-            faces[r, f] = jnp.dot(stage[...], sel[f], preferred_element_type=F32).astype(BF)
+            rows_of = [face_slot(slot_at, f, k) for k in range(NPOS)]
+            if f < 2:
+                for g in range(2):
+                    for i in range(CHUNKS):
+                        mixed = None
+                        for k in range(SIDE):
+                            v = chunk(src, rows_of[g * SIDE + k], i)
+                            v = turn(v, SIDE * k - f * (SQ - SIDE))
+                            mixed = v if k == 0 else jnp.where(masks[5 + k] > 0.5, v, mixed)
+                        faces[r, f, g * CHUNKS + i] = mixed
+            else:
+                i = 0 if f == 2 else CHUNKS - 1
+                for k in range(NPOS // 2):
+                    a, b = chunk(src, rows_of[2 * k], i), chunk(src, rows_of[2 * k + 1], i)
+                    if f == 2:
+                        b = turn(b, SQ)
+                    else:
+                        a = turn(a, SQ)
+                    faces[r, f, k] = jnp.where(low_half, a, b)
             if r == 0 and f == 0:
                 pl.semaphore_wait(barrier, n - 1)
 
@@ -181,21 +211,30 @@
             def _():
                 face_copy(r, f).wait_recv()
 
-            stage[...] = lax.dot_general(
-                halo[r, f], sel[f], (((1,), (1,)), ((), ())), preferred_element_type=F32
-            ).astype(BF)
             for k in range(NPOS):
-                dst[slots + 1 + f * NPOS + k] = stage[
-                    k // 2 * chans : (k // 2 + 1) * chans, k % 2 * VOL : (k % 2 + 1) * VOL
-                ]
+                row = slots + 1 + f * NPOS + k
+                if f < 2:
+                    for i in range(CHUNKS):
+                        v = halo[r, f, k // SIDE * CHUNKS + i]
+                        v = turn(v, f * (SQ - SIDE) - SIDE * (k % SIDE))
+                        dst[row, :, i * LANES : (i + 1) * LANES] = v
+                else:
+                    i = 0 if f == 2 else CHUNKS - 1
+                    v = halo[r, f, k // 2]
+                    if k % 2 != f - 2:
+                        v = turn(v, SQ)
+                    dst[row, :, i * LANES : (i + 1) * LANES] = v
 
     def conv(r, base, src, finish):
         w = fine_w[r]
         w_near, w_far = w[:, : 3 * chans], w[:, 3 * chans :]
 
         def near_pass(j, c):
-            own = src[j]
-            taps = [own] + [tap(d, own, src[nb[d, j]], masks) for d in (0, 1)]
+            taps = [
+                src[j],
+                side_tap(src, j, nb[0, j], 1, SIDE, keep[0]),
+                side_tap(src, j, nb[1, j], -1, SIDE, keep[1]),
+            ]
             acc[j] = base[j].astype(F32) + jnp.dot(
                 w_near, jnp.concatenate(taps, axis=0), preferred_element_type=F32
             )
@@ -205,8 +244,11 @@
         take_faces(r, src)
 
         def far_pass(j, c):
-            own = src[j]
-            taps = [tap(d, own, src[nb[d, j]], masks) for d in (2, 3, 4, 5)]
+            taps = [
+                side_tap(src, j, nb[2, j], SIDE, SIDE, keep[2]),
+                side_tap(src, j, nb[3, j], -SIDE, SIDE, keep[3]),
+                *depth_taps(src, j, nb[4, j], nb[5, j], low_half),
+            ]
             finish(
                 j,
                 acc[j] + jnp.dot(
@@ -218,7 +260,6 @@
         lax.fori_loop(0, slots, far_pass, 0, unroll=2)
 
     send_faces(0, ext)
-    loads[1].wait()
 
     pooled[slots] = jnp.zeros((8, chans), F32)
     pm = pool[...]
@@ -242,7 +283,7 @@
     oct_lane = lax.broadcasted_iota(jnp.int32, (m * 8, width), 1) // chans
     wide = jnp.where(oct_row == oct_lane, wide, 0.0)
     flat = jnp.sum(wide.reshape(m, 8, width), axis=1).astype(BF)
-    loads[2].wait()
+    loads[0].wait()
     ci = jnp.zeros((cells, wide_c), F32)
     for p in range(8):
         ci = ci + jnp.dot(
@@ -315,7 +356,7 @@
         lax.broadcasted_iota(jnp.int32, (wide_c, wide_c), 0) // group
         == lax.broadcasted_iota(jnp.int32, (wide_c, wide_c), 1) // group
     ).astype(F32)
-    for c in loads[3:]:
+    for c in loads[1:]:
         c.wait()
     for d in range(n_my):
         if d:
@@ -385,9 +426,11 @@
     whole = jnp.concatenate([result[j] for j in range(n_my)], axis=1)
     co = (whole + jnp.concatenate([coarse[0], coarse[1]], axis=0)).astype(BF)
     cof = co.astype(F32)
-    for q in range(cells):
-        z, x, y = q // 4, q // 2 % 2, q % 2
-        coarse_out[(z * 2 + y) * 2 + x : (z * 2 + y) * 2 + x + 1, :] = cof[q : q + 1]
+    for z in range(2):
+        for y in range(2):
+            q = z * 4 + y
+            pair = jnp.concatenate([cof[q : q + 1], cof[q + 2 : q + 3]], axis=0)
+            coarse_out[z, y] = pair.astype(BF)
     wide = jnp.dot(co, up[...], preferred_element_type=F32)
     for p in range(8):
         for q in range(cells):
@@ -420,7 +463,7 @@
     send_faces(2, ext2)
 
     def last_done(j, value):
-        out[j] = jnp.where(j < count, value, 0.0).astype(BF)
+        out[j] = value.astype(BF)
 
     conv(2, level, ext2, last_done)
 
@@ -434,7 +477,7 @@
     major, minor = lax.axis_index("mx"), lax.axis_index("my")
     cells = (RZ // 2) * (RY // 2) * (RX // 2)
     width = down_weight.shape[1]
-    masks, sel, pool, spread, octs = constants(chans)
+    masks, pool, spread, octs = constants(chans)
     ids = jnp.arange(slots, dtype=jnp.int32)
     lin = ((coords[0] - major * RZ) * RY + coords[1] - minor * RY) * RX + coords[2]
     lin = jnp.where(ids < counts[0], lin, -1)
@@ -445,19 +488,17 @@
     weight_t = coarse_weight.T
     held = [
         pltpu.VMEM(a.shape, a.dtype)
-        for a in (masks, sel, octs, down_weight, up_weight, weight_t)
+        for a in (octs, down_weight, up_weight, weight_t)
     ]
     ext = pltpu.VMEM((slots + 1 + 4 * NPOS, chans, VOL), BF)
     ext_small = pltpu.VMEM((slots, chans, VOL), BF)
-    pairs = NPOS // 2 * chans
     dma = pltpu.SemaphoreType.DMA
     scratch = held + [
         ext, ext,
         pltpu.VMEM((slots, chans, VOL), F32),
         ext_small,
-        pltpu.VMEM((pairs, 2 * VOL), BF),
-        pltpu.VMEM((3, 4, pairs, 2 * SQ), BF),
-        pltpu.VMEM((3, 4, pairs, 2 * SQ), BF),
+        pltpu.VMEM((3, 4, NPOS // 2, chans, LANES), BF),
+        pltpu.VMEM((3, 4, NPOS // 2, chans, LANES), BF),
         pltpu.VMEM((slots + 1, 8, chans), F32),
         pltpu.VMEM((8 * cells * 8, chans), F32),
         pltpu.VMEM((2, cells // 2, width), F32),
@@ -470,21 +511,22 @@
         pltpu.VMEM((8 * cells, 1, 8 * chans), F32),
         pltpu.SMEM((6, slots), jnp.int32),
         pltpu.SMEM((slots,), jnp.int32),
-        dma((6,)), dma((3, 4)), dma((3, 4)), dma((n,)), dma((n,)),
+        dma((4,)), dma((3, 4)), dma((3, 4)), dma((n,)), dma((n,)),
         dma((3, n_my)), dma((3, n_my)), dma((n_my,)), dma((n_my,)),
     ]
     fine, out = pl.pallas_call(
         functools.partial(level_kernel, slots, chans, cells),
-        out_shape=(sds(features.shape, BF), sds((cells, width), F32)),
-        in_specs=[SM] * 4 + [VM] * 6 + [pl.BlockSpec(memory_space=pl.ANY)] * 6,
+        out_shape=(sds(features.shape, BF), sds((RZ // 2, RY // 2, RX // 2, width), BF)),
+        in_specs=[SM] * 4 + [VM] * 7 + [pl.BlockSpec(memory_space=pl.ANY)] * 4,
         out_specs=(VM, VM),
         scratch_shapes=scratch,
         compiler_params=pltpu.CompilerParams(collective_id=0, has_side_effects=True),
     )(
         slot_at, coords, counts, neighbours, features, fine_weights, norm_gain[None, :],
-        norm_bias[None, :], pool, spread, masks, sel, octs, down_weight, up_weight, weight_t,
+        norm_bias[None, :], pool, spread, masks, octs, down_weight, up_weight, weight_t,
     )
-    return fine, out.astype(BF).reshape(RZ // 2, RY // 2, RX // 2, width)
+    fine = jnp.where((ids < counts[0])[:, None, None], fine, jnp.zeros_like(fine))
+    return fine, out
 
 
 def solution(mesh):

time: 67.8 us -> 63.1 us (0.931)
  Pallas kernels: 62 us -> 57.3 us
  local copies, waits for them, and re-layouts: 2.93 us -> 1.27 us
  other arithmetic: 1.32 us -> 2.96 us
    pallas_call x1, Pallas kernels: 62 us -> 57.3 us  [local(): pl.pallas_call(functools.partial(level_kernel, slots, chans, cells), out_...]
    select_n x0 -> x1, other arithmetic: none -> 2.34 us  [local(): jnp.where((ids < counts[0])[:, None, None], fine, jnp.zeros_like(fine))]
    unnamed x3 -> x5, local copies, waits for them, and re-layouts: 2.32 us -> 1.27 us
    convert_element_type x1 -> x0, other arithmetic: 0.7 us -> none  [local(): return (fine, out.astype(BF).reshape(RZ // 2, RY // 2, RX // 2, width))]
where the time goes in v3:
time: 63.1 us; the launch traced here: 62.9 us
  Pallas kernels  57.3 us (91%)
  other arithmetic  2.96 us (5%)
  between operations  1.31 us (2%)
  local copies, waits for them, and re-layouts  1.27 us (2%)
    pallas_call x1, Pallas kernels, local(): pl.pallas_call(functools.partial(level_kernel, slots, chans, cells), out_...  57.3 us
    select_n x1, other arithmetic, local(): jnp.where((ids < counts[0])[:, None, None], fine, jnp.zeros_like(fine))  2.34 us
    unnamed x5, local copies, waits for them, and re-layouts  1.27 us

profile of v3, /device:TPU:0, one launch (start us, length us, event | category | flops | bytes accessed | tf_op | source)
XLA Modules:
  0.0 62.9 jit_solution(13038315118904359192)
XLA Ops:
  1.3 0.0 copy-start
  1.3 0.7 %copy-done = s32[3,32]{1,0:T(4,128)S(1)} copy-done((s32[3,32]{1,0:T(4,128)S(1)}, s32[3,32]{1,0:T(4,128)}, u32[]{:S(2)}) %copy-start) | copy-done | bytes 408
  2.0 0.1 select_reduce_fusion
  2.1 0.5 broadcast_add_fusion.slot_at
  2.6 57.3 %shard_map.149 = (bf16[32,32,512]{2,1,0:T(8,128)(2,1)}, bf16[2,2,2,256]{3,2,1,0:T(2,128)(2,1)}) custom-call(s32[64]{0:T(128)} %broadcast_add_fusion.slot_at, s32[3,32]{1,0:T(4,128)} %coords.1, s32[1]{0:T(128)} %copy.17.counts, s32[6,32]{1,0:T(8,128)} %neighbours.1, bf16[32,32,512]{2,1,0:T(8,128)(2,1)} %feat.1, bf16[3,32,224]{2,1,0:T(8,128)(2,1)} %fine_w.1, ...), custom_call_target="tpu_custom_call" | custom-call | tf_op jit(solution)/shard_map/pallas_call | solution.py:517
  59.9 0.0 copy-start.1
  59.9 2.3 %broadcast_select_fusion = bf16[32,32,512]{2,1,0:T(8,128)(2,1)} fusion(bf16[32,32,512]{2,1,0:T(8,128)(2,1)} %get-tuple-element.4, pred[32]{0:T(512)(128)(4,1)S(1)} %iota_compare_fusion.1), kind=kLoop, calls=%fused_computation | loop fusion | flops 524288 | bytes 2097184 | tf_op jit(solution)/shard_map/jit(_where)/select_n | solution.py:528
  62.3 0.0 copy-done.1
  62.3 0.6 copy.18
  (3 shorter events, 0.0 us)
Async XLA Ops:
  1.3 0.7 %copy-start = (s32[3,32]{1,0:T(4,128)S(1)}, s32[3,32]{1,0:T(4,128)}, u32[]{:S(2)}) copy-start(s32[3,32]{1,0:T(4,128)} %coords.1) | copy-start | bytes 1156
  59.9 2.3 %copy-start.1 = (bf16[2,2,2,256]{3,2,1,0:T(2,128)(2,1)S(1)}, bf16[2,2,2,256]{3,2,1,0:T(2,128)(2,1)}, u32[]{:S(2)}) copy-start(bf16[2,2,2,256]{3,2,1,0:T(2,128)(2,1)} %get-tuple-element.9) | copy-start | bytes 12292

commit v4 on v3

--- a/solution.py
+++ b/solution.py
@@ -16,6 +16,7 @@
 VOL = SIDE**3
 SQ = SIDE * SIDE
 NPOS = 16
+UNROLL = 8
 LANES = 2 * SQ
 CHUNKS = VOL // LANES
 norm_eps = 1e-05
@@ -46,7 +47,8 @@
 
 
 def silu(x):
-    return x * jax.nn.sigmoid(x)
+    h = 0.5 * x
+    return h * jnp.tanh(h) + h
 
 
 def face_slot(slot_at, face, k):
@@ -133,9 +135,7 @@
     first_slot = me * slots
     count = counts[0]
 
-    def begin(j, c):
-        s = silu(feat[j].astype(F32)).astype(BF)
-        ext[j] = s
+    def tables(j):
         z = coords[0, j] - mx * RZ
         y = coords[1, j] - my * RY
         x = coords[2, j]
@@ -149,9 +149,13 @@
         q = (z // 2 * 2 + x // 2) * 2 + y // 2
         p = z % 2 * 4 + y % 2 * 2 + x % 2
         tgt[j] = jnp.clip(jnp.where(j < count, p * cells + q, 0), 0, 8 * cells - 1)
+
+    def begin(j, c):
+        s = silu(feat[j].astype(F32)).astype(BF)
+        ext[j] = s
         return c
 
-    lax.fori_loop(0, slots, begin, 0, unroll=2)
+    lax.fori_loop(0, slots, begin, 0, unroll=UNROLL)
     keep = [masks[i] > 0.5 for i in range(5)]
     low_half = keep[4]
 
@@ -230,6 +234,8 @@
         w_near, w_far = w[:, : 3 * chans], w[:, 3 * chans :]
 
         def near_pass(j, c):
+            if r == 0:
+                tables(j)
             taps = [
                 src[j],
                 side_tap(src, j, nb[0, j], 1, SIDE, keep[0]),
@@ -240,7 +246,7 @@
             )
             return c
 
-        lax.fori_loop(0, slots, near_pass, 0, unroll=2)
+        lax.fori_loop(0, slots, near_pass, 0, unroll=UNROLL)
         take_faces(r, src)
 
         def far_pass(j, c):
@@ -257,7 +263,7 @@
             )
             return c
 
-        lax.fori_loop(0, slots, far_pass, 0, unroll=2)
+        lax.fori_loop(0, slots, far_pass, 0, unroll=UNROLL)
 
     send_faces(0, ext)
 
@@ -451,7 +457,7 @@
         ext[j] = silu(f.astype(F32)).astype(BF)
         return c
 
-    lax.fori_loop(0, slots, join, 0, unroll=2)
+    lax.fori_loop(0, slots, join, 0, unroll=UNROLL)
     send_faces(1, ext)
 
     def second_done(j, value):

time: 63.1 us -> 52.1 us (0.83)
  Pallas kernels: 57.3 us -> 46.3 us
    pallas_call x1, Pallas kernels: 57.3 us -> 46.3 us  [local(): pl.pallas_call(functools.partial(level_kernel, slots, chans, cells), out_...]
where the time goes in v4:
time: 52.1 us; the launch traced here: 51.9 us
  Pallas kernels  46.3 us (89%)
  other arithmetic  2.96 us (6%)
  between operations  1.31 us (3%)
  local copies, waits for them, and re-layouts  1.27 us (2%)
    pallas_call x1, Pallas kernels, local(): pl.pallas_call(functools.partial(level_kernel, slots, chans, cells), out_...  46.3 us
    select_n x1, other arithmetic, local(): jnp.where((ids < counts[0])[:, None, None], fine, jnp.zeros_like(fine))  2.34 us
    unnamed x5, local copies, waits for them, and re-layouts  1.27 us

profile of v4, /device:TPU:0, one launch (start us, length us, event | category | flops | bytes accessed | tf_op | source)
XLA Modules:
  0.0 51.9 jit_solution(8879522477527984864)
XLA Ops:
  1.3 0.0 copy-start
  1.3 0.7 %copy-done = s32[3,32]{1,0:T(4,128)S(1)} copy-done((s32[3,32]{1,0:T(4,128)S(1)}, s32[3,32]{1,0:T(4,128)}, u32[]{:S(2)}) %copy-start) | copy-done | bytes 408
  2.0 0.1 select_reduce_fusion
  2.1 0.5 broadcast_add_fusion.slot_at
  2.6 46.3 %shard_map.149 = (bf16[32,32,512]{2,1,0:T(8,128)(2,1)}, bf16[2,2,2,256]{3,2,1,0:T(2,128)(2,1)}) custom-call(s32[64]{0:T(128)} %broadcast_add_fusion.slot_at, s32[3,32]{1,0:T(4,128)} %coords.1, s32[1]{0:T(128)} %copy.17.counts, s32[6,32]{1,0:T(8,128)} %neighbours.1, bf16[32,32,512]{2,1,0:T(8,128)(2,1)} %feat.1, bf16[3,32,224]{2,1,0:T(8,128)(2,1)} %fine_w.1, ...), custom_call_target="tpu_custom_call" | custom-call | tf_op jit(solution)/shard_map/pallas_call | solution.py:523
  48.9 0.0 copy-start.1
  48.9 2.3 %broadcast_select_fusion = bf16[32,32,512]{2,1,0:T(8,128)(2,1)} fusion(bf16[32,32,512]{2,1,0:T(8,128)(2,1)} %get-tuple-element.4, pred[32]{0:T(512)(128)(4,1)S(1)} %iota_compare_fusion.1), kind=kLoop, calls=%fused_computation | loop fusion | flops 524288 | bytes 2097184 | tf_op jit(solution)/shard_map/jit(_where)/select_n | solution.py:534
  51.3 0.0 copy-done.1
  51.3 0.6 %copy.18 = bf16[2,2,2,256]{3,2,1,0:T(2,128)(2,1)} copy(bf16[2,2,2,256]{3,2,1,0:T(2,128)(2,1)S(1)} %copy-done.1) | data formatting | bytes 8192
  (3 shorter events, 0.0 us)
Async XLA Ops:
  1.3 0.7 %copy-start = (s32[3,32]{1,0:T(4,128)S(1)}, s32[3,32]{1,0:T(4,128)}, u32[]{:S(2)}) copy-start(s32[3,32]{1,0:T(4,128)} %coords.1) | copy-start | bytes 1156
  48.9 2.3 %copy-start.1 = (bf16[2,2,2,256]{3,2,1,0:T(2,128)(2,1)S(1)}, bf16[2,2,2,256]{3,2,1,0:T(2,128)(2,1)}, u32[]{:S(2)}) copy-start(bf16[2,2,2,256]{3,2,1,0:T(2,128)(2,1)} %get-tuple-element.9) | copy-start | bytes 12292
